TPU v7x, 128 devices: a whole 4x4x4 slice. The times are simulated.
128 devices in a mesh: dom: 8 (over y, core), narrow: 16 (over z, x).
Axes of the slice: x: 4, y: 4, z: 4, core: 2. Of those that a mesh axis runs over, the one named last changes fastest.
Arguments:
- feats: bfloat16 [131072, 768], P(('dom', 'narrow')), may hold values from -21 to 21
- node_type: int32 [1024], P('dom'), may hold values from 0 to 2
- tiles: int32 [1024, 4], P('dom'), may hold values from 0 to 127, as said below
- relation: int32 [1024, 4], P(('dom', 'narrow')), may hold values from 0 to 4
- neg_sched: int32 [128, 8], P('dom'), may hold values from 0 to 7
- w_query: bfloat16 [3, 768, 768], replicated, may hold values from -0.21875 to 0.21875
- w_key: bfloat16 [3, 768, 768], replicated, may hold values from -0.21875 to 0.21875
- w_value: bfloat16 [3, 768, 768], replicated, may hold values from -0.21875 to 0.21875
- w_out: bfloat16 [3, 768, 768], replicated, may hold values from -0.21875 to 0.21875
- rel_att: bfloat16 [5, 8, 96, 96], replicated, may hold values from -0.625 to 0.625
- rel_msg: bfloat16 [5, 8, 96, 96], replicated, may hold values from -0.625 to 0.625
- rel_prior: float32 [5, 8], replicated, may hold values from 0.5 to 2
- skip_gate: float32 [3], replicated, may hold values from -2 to 2
- pos_view: bfloat16 [131072, 768], P(('dom', 'narrow')), may hold values from -6 to 6
- type_weight: float32 [3], replicated, may hold values from 0.5 to 2
Outputs:
- embedding: bfloat16 [131072, 768], P(('dom', 'narrow'))
- node_loss: float32 [131072], P(('dom', 'narrow'))
- mean_loss: float32 [], replicated
Inputs may be any that keep to these rules, and one draw needn't show every extreme that they name: `tiles`: values are block numbers within the target block's group: owner lane times 8 plus the owner's local block. Among the 32 entries of one device's target blocks, at most 3 name blocks of any one lane.
All inputs are finite; a program needn't handle non-finite values.
Results may differ from a plain program's by a relative error of at most 0.008.
The roundings to bfloat16 on the way count: a program that leaves them out, or rounds other values in their place, can miss the bound.
Values may be sent and summed in bfloat16 or wider, within the bound.
A program may use at most 128 MiB of HBM per device.

v0:
```python
import math

import jax
import jax.numpy as jnp
from jax import lax
from jax.sharding import Mesh
from jax.sharding import PartitionSpec as P

D = 768
HEADS = 8
DH = 96
TILE = 128
NT = 4
NARROW = ("narrow_0", "narrow_1")
DOM_NARROW = ("dom_0", "dom_1", "narrow_0", "narrow_1")
DOM = ("dom_0", "dom_1")


def cut_along(array, dim, count):
    before, after = (array.shape[:dim], array.shape[dim + 1 :])
    return jnp.moveaxis(array.reshape(*before, count, -1, *after), dim, 0)


def cut_rows(length, count):
    turn = length // count
    if turn >= 8:
        turn -= turn % 8
    return [turn * k for k in range(1, count)]


def in_order(blocks, dim):
    blocks = jnp.moveaxis(blocks, 0, dim)
    dims = blocks.shape
    return blocks.reshape(*dims[:dim], dims[dim] * dims[dim + 1], *dims[dim + 2 :])


def cut_exchange(array, axis, pieces, split_dim, concat_dim):
    blocks = cut_along(array, split_dim, lax.axis_size(axis))
    cut = max(range(1, max(2, blocks.ndim - 1)), key=lambda d: blocks.shape[d])
    done = []
    for piece in jnp.split(blocks, cut_rows(blocks.shape[cut], pieces), axis=cut):
        if piece.size:
            done.append(lax.all_to_all(piece, axis, split_axis=0, concat_axis=0, tiled=True))
    return in_order(jnp.concatenate(done, axis=cut), concat_dim)


def shifted(array, axis, by):
    count = lax.axis_size(axis)
    return lax.ppermute(array, axis, [(i, (i + by) % count) for i in range(count)])


def over_axes(array, axes):
    for axis in axes:
        array = lax.psum(array, axis)
    return array


def shards(
    feats,
    node_type,
    tiles,
    relation,
    neg_sched,
    w_query,
    w_key,
    w_value,
    w_out,
    rel_att,
    rel_msg,
    rel_prior,
    skip_gate,
    pos_view,
    type_weight,
):
    lane_count = lax.axis_size(NARROW)
    my_lane = lax.axis_index(NARROW)
    nblocks = feats.shape[0] // TILE
    requests = nblocks * NT
    capacity = (requests + lane_count - 1) // lane_count + 1
    blocks = feats.reshape(nblocks, TILE, D)
    group_lists = tiles.reshape(lane_count, requests)
    owners = group_lists // nblocks
    local_tile = group_lists % nblocks
    position = jnp.arange(requests, dtype=jnp.int32)
    before = position[None, :] < position[:, None]
    same_owner = owners[:, :, None] == owners[:, None, :]
    rank_of = jnp.sum(jnp.logical_and(same_owner, before[None]).astype(jnp.int32), axis=2)
    my_tiles = lax.dynamic_index_in_dim(group_lists, my_lane, 0, keepdims=False)
    my_owners = lax.dynamic_index_in_dim(owners, my_lane, 0, keepdims=False)
    my_ranks = lax.dynamic_index_in_dim(rank_of, my_lane, 0, keepdims=False)
    own_types = lax.dynamic_slice_in_dim(node_type, my_lane * nblocks, nblocks)
    source_types = node_type[my_tiles].reshape(nblocks, NT)
    columns = blocks.shape[2]
    slot_ids = jnp.arange(capacity, dtype=jnp.int32)
    chosen = jnp.logical_and(
        (owners == my_lane)[:, :, None], rank_of[:, :, None] == slot_ids[None, None, :]
    )
    send_index = jnp.sum(chosen.astype(jnp.int32) * local_tile[:, :, None], axis=1)
    outgoing = blocks[send_index]
    incoming = cut_exchange(outgoing, NARROW, 2, 0, 0)
    fetched = incoming.reshape(lane_count * capacity, TILE, columns)[
        my_owners * capacity + my_ranks
    ]
    fetched = fetched.reshape(nblocks, NT, TILE, columns)

    def attend(inputs):
        own_rows, type_id, src_tiles, src_types, rel_ids = inputs
        query_rows = jnp.dot(own_rows, w_query[type_id], preferred_element_type=jnp.float32).astype(
            jnp.bfloat16
        )
        src_keys = jnp.einsum(
            "jmd,jde->jme", src_tiles, w_key[src_types], preferred_element_type=jnp.float32
        ).astype(jnp.bfloat16)
        src_values = jnp.einsum(
            "jmd,jde->jme", src_tiles, w_value[src_types], preferred_element_type=jnp.float32
        ).astype(jnp.bfloat16)
        keyed_rows = jnp.einsum(
            "jmhd,jhde->jmhe",
            src_keys.reshape(NT, TILE, HEADS, DH),
            rel_att[rel_ids],
            preferred_element_type=jnp.float32,
        ).astype(jnp.bfloat16)
        message = jnp.einsum(
            "jmhd,jhde->jmhe",
            src_values.reshape(NT, TILE, HEADS, DH),
            rel_msg[rel_ids],
            preferred_element_type=jnp.float32,
        ).astype(jnp.bfloat16)
        scores = jnp.einsum(
            "ihd,jmhd->hijm",
            query_rows.reshape(TILE, HEADS, DH),
            keyed_rows,
            preferred_element_type=jnp.float32,
        )
        prior_scale = jnp.transpose(rel_prior[rel_ids]) / math.sqrt(DH)
        scores = (scores * prior_scale[:, None, :, None]).reshape(HEADS, TILE, NT * TILE)
        highest = jnp.max(scores, axis=2, keepdims=True)
        exponent = jnp.exp(scores - highest)
        attention = (exponent / jnp.sum(exponent, axis=2, keepdims=True)).astype(jnp.bfloat16)
        merged = jnp.einsum(
            "hin,nhe->ihe",
            attention,
            message.reshape(NT * TILE, HEADS, DH),
            preferred_element_type=jnp.float32,
        )
        activated = jax.nn.gelu(merged.reshape(TILE, D), approximate=False).astype(jnp.bfloat16)
        projected = jnp.dot(activated, w_out[type_id], preferred_element_type=jnp.float32)
        mix_gate = jax.nn.sigmoid(skip_gate[type_id])
        return (mix_gate * projected + (1.0 - mix_gate) * own_rows.astype(jnp.float32)).astype(
            jnp.bfloat16
        )

    embedding_blocks = lax.map(attend, (blocks, own_types, fetched, source_types, relation))
    steps_count = lane_count // 2
    my_sched = lax.dynamic_index_in_dim(neg_sched, my_lane, 0, keepdims=False)
    gathered_negs = []
    for offset in range(1, steps_count + 1):
        chosen_block = lax.dynamic_index_in_dim(
            embedding_blocks, my_sched[offset - 1], 0, keepdims=False
        )
        gathered_negs.append(shifted(chosen_block, NARROW, offset))
    negatives = jnp.stack(gathered_negs).reshape(steps_count * TILE, D)
    offsets = jnp.arange(1, steps_count + 1, dtype=jnp.int32)
    sender_lane = (my_lane - offsets) % lane_count
    neg_blocks = neg_sched[sender_lane, offsets - 1]
    neg_types = jnp.repeat(
        node_type[sender_lane * nblocks + neg_blocks], TILE, total_repeat_length=steps_count * TILE
    )
    row_types = jnp.repeat(own_types, TILE, total_repeat_length=nblocks * TILE)
    embedding = embedding_blocks.reshape(nblocks * TILE, D)
    positive = jnp.einsum(
        "nd,nd->n", embedding, pos_view, preferred_element_type=jnp.float32
    ) / math.sqrt(D)
    neg_logits = jnp.einsum(
        "nd,md->nm", embedding, negatives, preferred_element_type=jnp.float32
    ) / math.sqrt(D)
    neg_logits = jnp.where(row_types[:, None] == neg_types[None, :], neg_logits, -jnp.inf)
    highest = jnp.maximum(positive, jnp.max(neg_logits, axis=1))
    denominator = jnp.exp(positive - highest) + jnp.sum(
        jnp.exp(neg_logits - highest[:, None]), axis=1
    )
    node_loss = highest + jnp.log(denominator) - positive
    type_match = (
        row_types[:, None] == jnp.arange(type_weight.shape[0], dtype=jnp.int32)[None, :]
    ).astype(jnp.float32)
    row_weight = jnp.sum(type_match * type_weight[None, :], axis=1)
    overall = over_axes(jnp.sum(row_weight * node_loss), DOM_NARROW)
    mean_loss = overall / (node_loss.shape[0] * lax.axis_size(DOM) * lax.axis_size(NARROW))
    return (embedding, node_loss, mean_loss)


def solution(mesh):
    finer = Mesh(mesh.devices.reshape(4, 2, 4, 4), ("dom_0", "dom_1", "narrow_0", "narrow_1"))
    in_specs = (
        P(DOM_NARROW, None),
        P(DOM),
        P(DOM, None),
        P(DOM_NARROW, None),
        P(DOM, None),
        P(),
        P(),
        P(),
        P(),
        P(),
        P(),
        P(),
        P(),
        P(DOM_NARROW, None),
        P(),
    )
    out_specs = (P(DOM_NARROW, None), P(DOM_NARROW), P())
    return jax.shard_map(
        shards, mesh=finer, in_specs=in_specs, out_specs=out_specs, check_vma=False
    )
```

profile of v0, /device:TPU:1, one launch (start us, length us, event | category | flops | bytes accessed | tf_op | source)
XLA Modules:
  0.0 551.7 jit_solution(5968654400058325688)
XLA Ops:
  2.4 7.8 %gather_fusion.5 = bf16[48,128,768]{2,1,0:T(8,128)(2,1)} fusion(bf16[8,128,768]{2,1,0:T(8,128)(2,1)} %bitcast.340, s32[1024]{0:T(1024)S(1)} %get-tuple-element.239), kind=kCustom, calls=%fused_computation.5 | custom fusion | bytes 18874560 | tf_op jit(solution)/shard_map/gather | solution.py:99
  10.2 6.8 %fusion.92 = (bf16[16,1,3,64,768]{4,3,2,1,0:T(8,128)(2,1)S(1)}, bf16[16,1,3,64,768]{4,3,2,1,0:T(8,128)(2,1)}) fusion(bf16[16,1,3,128,768]{4,3,2,1,0:T(8,128)(2,1)} %bitcast.344), kind=kLoop, calls=%fused_computation.163 | loop fusion | bytes 18874368 | tf_op jit(solution)/shard_map/split | solution.py:41
  17.0 63.6 %all_to_all.10 = bf16[16,1,3,64,768]{4,3,2,1,0:T(8,128)(2,1)} all-to-all(bf16[16,1,3,64,768]{4,3,2,1,0:T(8,128)(2,1)S(1)} %get-tuple-element.200), channel_id=1, replica_groups=mesh['dom_0'=4,'dom_1'=2,'narrow_0'=4,'narrow_1'=4] {'narrow_0','narrow_1'}, dimensions={0} | all-to-all | bytes 9437184 | tf_op jit(solution)/shard_map/all_to_all | solution.py:43
  80.7 4.7 all-to-all-start.1
  106.8 10.5 %select_select_fusion = (s32[1024]{0:T(1024)}, s32[1024]{0:T(1024)S(1)}) fusion(s32[]{:T(128)} %bitcast.53, s32[]{:T(128)} %bitcast.52, s32[]{:T(128)} %bitcast.51, s32[]{:T(128)} %bitcast.50, s32[]{:T(128)} %bitcast.49, s32[]{:T(128)} %bitcast.48, s32[]{:T(128)} %bitcast.47, s32[]{:T(128)} %bitcast.46, s32[]{:T(128)} %bitcast.42, s32[]{:T(128)} %bitcast.41, ...), kind=kLoop, calls=%fused_computation.123 | loop fusion | flops 31744 | bytes 8256 | tf_op jit(solution)/shard_map/jit(_take)/select_n | solution.py:166
  117.9 34.6 %all-to-all-done.1 = bf16[16,1,3,64,768]{4,3,2,1,0:T(8,128)(2,1)} async-done(((bf16[16,1,3,64,768]{4,3,2,1,0:T(8,128)(2,1)}), bf16[16,1,3,64,768]{4,3,2,1,0:T(8,128)(2,1)}, u32[]{:S(2)}, u32[]{:S(2)}) %all-to-all-start.1) | async-done | bytes 4718624 | tf_op jit(solution)/shard_map/all_to_all | solution.py:43
  152.6 7.6 %pad_maximum_fusion = bf16[16,1,3,128,768]{4,3,2,1,0:T(8,128)(2,1)} fusion(bf16[16,1,3,64,768]{4,3,2,1,0:T(8,128)(2,1)} %all-to-all-done.1, bf16[16,1,3,64,768]{4,3,2,1,0:T(8,128)(2,1)} %all_to_all.10), kind=kLoop, calls=%fused_computation.80 | loop fusion | flops 18874368 | bytes 18874368 | tf_op jit(solution)/shard_map/concatenate | solution.py:44
  160.2 7.5 %gather_fusion.6 = bf16[32,128,768]{2,1,0:T(8,128)(2,1)} fusion(bf16[48,128,768]{2,1,0:T(8,128)(2,1)} %bitcast.346, s32[1024]{0:T(1024)S(1)} %pad_clamp_fusion.4), kind=kCustom, calls=%fused_computation.6 | custom fusion | bytes 12583040 | tf_op jit(solution)/shard_map/gather | solution.py:101
  167.6 307.8 %while.12 = (s32[]{:T(128)}, bf16[8,128,768]{2,1,0:T(8,128)(2,1)}, s32[8]{0:T(128)}, f32[3]{0:T(128)}, s32[8,4]{1,0:T(8,128)}, /*index=5*/bf16[5,8,96,96]{3,2,1,...) while((s32[]{:T(128)}, bf16[8,128,768]{2,1,0:T(8,128)(2,1)}, ...), condition=%wide.region_5.6_spmd, body=%wide.region_2.5_spmd.sunk | while | flops 1874493440 | bytes 76776536 | solution.py:153
  178.4 3.4 convolution_convert_fusion.6
  188.6 5.0 gather_fusion.4
  193.6 3.4 convolution_convert_fusion.7
  198.6 3.9 fusion.142
  216.9 3.4 convolution_convert_fusion.6
  227.1 5.0 gather_fusion.4
  232.1 3.4 convolution_convert_fusion.7
  237.1 3.9 fusion.142
  255.4 3.4 convolution_convert_fusion.6
  265.6 5.0 gather_fusion.4
  270.5 3.4 convolution_convert_fusion.7
  275.6 3.9 fusion.142
  293.9 3.4 convolution_convert_fusion.6
  304.1 5.0 gather_fusion.4
  309.0 3.4 convolution_convert_fusion.7
  314.0 3.9 fusion.142
  332.3 3.4 convolution_convert_fusion.6
  342.5 5.0 gather_fusion.4
  347.5 3.4 convolution_convert_fusion.7
  352.5 3.9 fusion.142
  370.8 3.4 convolution_convert_fusion.6
  381.0 5.0 gather_fusion.4
  386.0 3.4 convolution_convert_fusion.7
  391.0 3.9 fusion.142
  409.3 3.4 convolution_convert_fusion.6
  419.5 5.0 gather_fusion.4
  424.5 3.4 convolution_convert_fusion.7
  429.5 3.9 fusion.142
  447.8 3.4 convolution_convert_fusion.6
  458.0 5.0 gather_fusion.4
  462.9 3.4 convolution_convert_fusion.7
  467.9 3.9 fusion.142
  483.7 5.7 %collective-permute-done = bf16[128,768]{1,0:T(8,128)(2,1)S(1)} collective-permute-done((bf16[128,768]{1,0:T(8,128)(2,1)S(1)}, bf16[128,768]{1,0:T(8,128)(2,1)S(1)}, u32[]{:S(2)}, u32[]{:S(2)}) %collective-permute-start) | collective-permute-done | bytes 196640 | tf_op jit(solution)/shard_map/ppermute | solution.py:49
  491.6 21.2 %collective-permute-done.3 = bf16[128,768]{1,0:T(8,128)(2,1)S(1)} collective-permute-done((bf16[128,768]{1,0:T(8,128)(2,1)S(1)}, bf16[128,768]{1,0:T(8,128)(2,1)S(1)}, u32[]{:S(2)}, u32[]{:S(2)}) %collective-permute-start.3) | collective-permute-done | bytes 196640 | tf_op jit(solution)/shard_map/ppermute | solution.py:49
  513.0 4.8 collective-permute-done.7
  522.0 9.4 %psum.28 = f32[]{:T(128)} all-reduce(f32[]{:T(128)} %get-tuple-element.192), channel_id=1, replica_groups=mesh['dom_0'=4,'dom_1'=2,'narrow_0'=4,'narrow_1'=4] {'dom_0'}, use_global_device_ids=true, to_apply=%region_10.12 | all-reduce | flops 1 | bytes 8 | tf_op jit(solution)/shard_map/psum | solution.py:54
  531.4 5.2 psum.29
  536.6 6.7 %psum.30 = f32[]{:T(128)} all-reduce(f32[]{:T(128)} %psum.29), channel_id=1, replica_groups=mesh['dom_0'=4,'dom_1'=2,'narrow_0'=4,'narrow_1'=4] {'narrow_0'}, use_global_device_ids=true, to_apply=%region_12.14 | all-reduce | flops 1 | bytes 8 | tf_op jit(solution)/shard_map/psum | solution.py:54
  543.3 6.6 %psum.31 = f32[]{:T(128)} all-reduce(f32[]{:T(128)} %psum.30), channel_id=1, replica_groups=mesh['dom_0'=4,'dom_1'=2,'narrow_0'=4,'narrow_1'=4] {'narrow_1'}, use_global_device_ids=true, to_apply=%region_13.15 | all-reduce | flops 1 | bytes 8 | tf_op jit(solution)/shard_map/psum | solution.py:54
  (354 shorter events, 185.6 us)
Async XLA Ops:
  0.6 84.7 %copy-start = (s32[16,8]{0,1:T(8,128)S(1)}, s32[16,8]{0,1:T(8,128)}, u32[]{:S(2)}) copy-start(s32[16,8]{0,1:T(8,128)} %param.27) | copy-start | bytes 1540
  80.7 15.4 %copy-start.2 = (s32[128]{0:T(128)S(1)}, s32[128]{0:T(128)}, u32[]{:S(2)}) copy-start(s32[128]{0:T(128)} %param.24) | copy-start | bytes 1540
  80.7 16.8 %copy-start.17 = (s32[8,4]{0,1:T(4,128)S(1)}, s32[8,4]{0,1:T(4,128)}, u32[]{:S(2)}) copy-start(s32[8,4]{0,1:T(4,128)} %param.26) | copy-start | bytes 388
  80.7 36.6 %copy-start.18 = (f32[3]{0:T(128)S(1)}, f32[3]{0:T(128)}, u32[]{:S(2)}) copy-start(f32[3]{0:T(128)} %param.37) | copy-start | bytes 40
  80.7 71.9 %all-to-all-start.1 = ((bf16[16,1,3,64,768]{4,3,2,1,0:T(8,128)(2,1)}), bf16[16,1,3,64,768]{4,3,2,1,0:T(8,128)(2,1)}, u32[]{:S(2)}, u32[]{:S(2)}) async-start(bf16[16,1,3,64,768]{4,3,2,1,0:T(8,128)(2,1)} %get-tuple-element.201), calls=%async_computation.1 | async-start | bytes 9437184 | tf_op jit(solution)/shard_map/all_to_all | solution.py:43
  117.3 42.9 %copy-start.11 = (s32[1024]{0:T(1024)}, s32[1024]{0:T(1024)S(1)}, u32[]{:S(2)}) copy-start(s32[1024]{0:T(1024)S(1)} %get-tuple-element.237) | copy-start | bytes 12292
  160.2 7.5 %copy-start.3 = (bf16[3,768,768]{2,1,0:T(8,128)(2,1)S(1)}, bf16[3,768,768]{2,1,0:T(8,128)(2,1)}, u32[]{:S(2)}) copy-start(bf16[3,768,768]{2,1,0:T(8,128)(2,1)} %param.29) | copy-start | bytes 10616836
  160.2 7.5 %copy-start.9 = (f32[5,8]{1,0:T(8,128)S(1)}, f32[5,8]{1,0:T(8,128)}, u32[]{:S(2)}) copy-start(f32[5,8]{1,0:T(8,128)} %param.34) | copy-start | bytes 484
  167.6 7.8 %copy-start.15 = (s32[8,4]{1,0:T(8,128)}, s32[8,4]{1,0:T(8,128)S(1)}, u32[]{:S(2)}) copy-start(s32[8,4]{1,0:T(8,128)S(1)} %get-tuple-element.386) | copy-start | bytes 388 | tf_op jit(solution)/shard_map/while
  198.6 3.9 copy-start.19
  198.6 7.5 %copy-start.4 = (bf16[3,768,768]{2,1,0:T(8,128)(2,1)S(1)}, bf16[3,768,768]{2,1,0:T(8,128)(2,1)}, u32[]{:S(2)}) copy-start(bf16[3,768,768]{2,1,0:T(8,128)(2,1)} %get-tuple-element.419) | copy-start | bytes 10616836 | tf_op jit(solution)/shard_map/while
  198.6 7.5 %copy-start.16 = (s32[8,4]{1,0:T(8,128)S(1)}, s32[8,4]{1,0:T(8,128)}, u32[]{:S(2)}) copy-start(s32[8,4]{1,0:T(8,128)} %copy-done.15) | copy-start | bytes 388 | tf_op jit(solution)/shard_map/while
  206.1 7.8 %copy-start.15 = (s32[8,4]{1,0:T(8,128)}, s32[8,4]{1,0:T(8,128)S(1)}, u32[]{:S(2)}) copy-start(s32[8,4]{1,0:T(8,128)S(1)} %get-tuple-element.386) | copy-start | bytes 388 | tf_op jit(solution)/shard_map/while
  237.1 3.9 copy-start.19
  237.1 7.5 %copy-start.4 = (bf16[3,768,768]{2,1,0:T(8,128)(2,1)S(1)}, bf16[3,768,768]{2,1,0:T(8,128)(2,1)}, u32[]{:S(2)}) copy-start(bf16[3,768,768]{2,1,0:T(8,128)(2,1)} %get-tuple-element.419) | copy-start | bytes 10616836 | tf_op jit(solution)/shard_map/while
  237.1 7.5 %copy-start.16 = (s32[8,4]{1,0:T(8,128)S(1)}, s32[8,4]{1,0:T(8,128)}, u32[]{:S(2)}) copy-start(s32[8,4]{1,0:T(8,128)} %copy-done.15) | copy-start | bytes 388 | tf_op jit(solution)/shard_map/while
  244.6 7.8 %copy-start.15 = (s32[8,4]{1,0:T(8,128)}, s32[8,4]{1,0:T(8,128)S(1)}, u32[]{:S(2)}) copy-start(s32[8,4]{1,0:T(8,128)S(1)} %get-tuple-element.386) | copy-start | bytes 388 | tf_op jit(solution)/shard_map/while
  275.5 3.9 copy-start.19
  275.5 7.5 %copy-start.4 = (bf16[3,768,768]{2,1,0:T(8,128)(2,1)S(1)}, bf16[3,768,768]{2,1,0:T(8,128)(2,1)}, u32[]{:S(2)}) copy-start(bf16[3,768,768]{2,1,0:T(8,128)(2,1)} %get-tuple-element.419) | copy-start | bytes 10616836 | tf_op jit(solution)/shard_map/while
  275.6 7.5 %copy-start.16 = (s32[8,4]{1,0:T(8,128)S(1)}, s32[8,4]{1,0:T(8,128)}, u32[]{:S(2)}) copy-start(s32[8,4]{1,0:T(8,128)} %copy-done.15) | copy-start | bytes 388 | tf_op jit(solution)/shard_map/while
  283.1 7.8 %copy-start.15 = (s32[8,4]{1,0:T(8,128)}, s32[8,4]{1,0:T(8,128)S(1)}, u32[]{:S(2)}) copy-start(s32[8,4]{1,0:T(8,128)S(1)} %get-tuple-element.386) | copy-start | bytes 388 | tf_op jit(solution)/shard_map/while
  314.0 7.5 %copy-start.4 = (bf16[3,768,768]{2,1,0:T(8,128)(2,1)S(1)}, bf16[3,768,768]{2,1,0:T(8,128)(2,1)}, u32[]{:S(2)}) copy-start(bf16[3,768,768]{2,1,0:T(8,128)(2,1)} %get-tuple-element.419) | copy-start | bytes 10616836 | tf_op jit(solution)/shard_map/while
  314.0 7.5 %copy-start.16 = (s32[8,4]{1,0:T(8,128)S(1)}, s32[8,4]{1,0:T(8,128)}, u32[]{:S(2)}) copy-start(s32[8,4]{1,0:T(8,128)} %copy-done.15) | copy-start | bytes 388 | tf_op jit(solution)/shard_map/while
  321.5 7.8 %copy-start.15 = (s32[8,4]{1,0:T(8,128)}, s32[8,4]{1,0:T(8,128)S(1)}, u32[]{:S(2)}) copy-start(s32[8,4]{1,0:T(8,128)S(1)} %get-tuple-element.386) | copy-start | bytes 388 | tf_op jit(solution)/shard_map/while
  352.5 7.5 %copy-start.4 = (bf16[3,768,768]{2,1,0:T(8,128)(2,1)S(1)}, bf16[3,768,768]{2,1,0:T(8,128)(2,1)}, u32[]{:S(2)}) copy-start(bf16[3,768,768]{2,1,0:T(8,128)(2,1)} %get-tuple-element.419) | copy-start | bytes 10616836 | tf_op jit(solution)/shard_map/while
  352.5 7.5 %copy-start.16 = (s32[8,4]{1,0:T(8,128)S(1)}, s32[8,4]{1,0:T(8,128)}, u32[]{:S(2)}) copy-start(s32[8,4]{1,0:T(8,128)} %copy-done.15) | copy-start | bytes 388 | tf_op jit(solution)/shard_map/while
  360.0 7.8 %copy-start.15 = (s32[8,4]{1,0:T(8,128)}, s32[8,4]{1,0:T(8,128)S(1)}, u32[]{:S(2)}) copy-start(s32[8,4]{1,0:T(8,128)S(1)} %get-tuple-element.386) | copy-start | bytes 388 | tf_op jit(solution)/shard_map/while
  391.0 7.5 %copy-start.4 = (bf16[3,768,768]{2,1,0:T(8,128)(2,1)S(1)}, bf16[3,768,768]{2,1,0:T(8,128)(2,1)}, u32[]{:S(2)}) copy-start(bf16[3,768,768]{2,1,0:T(8,128)(2,1)} %get-tuple-element.419) | copy-start | bytes 10616836 | tf_op jit(solution)/shard_map/while
  391.0 7.5 %copy-start.16 = (s32[8,4]{1,0:T(8,128)S(1)}, s32[8,4]{1,0:T(8,128)}, u32[]{:S(2)}) copy-start(s32[8,4]{1,0:T(8,128)} %copy-done.15) | copy-start | bytes 388 | tf_op jit(solution)/shard_map/while
  398.5 7.8 %copy-start.15 = (s32[8,4]{1,0:T(8,128)}, s32[8,4]{1,0:T(8,128)S(1)}, u32[]{:S(2)}) copy-start(s32[8,4]{1,0:T(8,128)S(1)} %get-tuple-element.386) | copy-start | bytes 388 | tf_op jit(solution)/shard_map/while
  429.4 7.5 %copy-start.4 = (bf16[3,768,768]{2,1,0:T(8,128)(2,1)S(1)}, bf16[3,768,768]{2,1,0:T(8,128)(2,1)}, u32[]{:S(2)}) copy-start(bf16[3,768,768]{2,1,0:T(8,128)(2,1)} %get-tuple-element.419) | copy-start | bytes 10616836 | tf_op jit(solution)/shard_map/while
  429.5 7.5 %copy-start.16 = (s32[8,4]{1,0:T(8,128)S(1)}, s32[8,4]{1,0:T(8,128)}, u32[]{:S(2)}) copy-start(s32[8,4]{1,0:T(8,128)} %copy-done.15) | copy-start | bytes 388 | tf_op jit(solution)/shard_map/while
  437.0 7.8 %copy-start.15 = (s32[8,4]{1,0:T(8,128)}, s32[8,4]{1,0:T(8,128)S(1)}, u32[]{:S(2)}) copy-start(s32[8,4]{1,0:T(8,128)S(1)} %get-tuple-element.386) | copy-start | bytes 388 | tf_op jit(solution)/shard_map/while
  467.9 7.5 %copy-start.4 = (bf16[3,768,768]{2,1,0:T(8,128)(2,1)S(1)}, bf16[3,768,768]{2,1,0:T(8,128)(2,1)}, u32[]{:S(2)}) copy-start(bf16[3,768,768]{2,1,0:T(8,128)(2,1)} %get-tuple-element.419) | copy-start | bytes 10616836 | tf_op jit(solution)/shard_map/while
  467.9 7.5 %copy-start.16 = (s32[8,4]{1,0:T(8,128)S(1)}, s32[8,4]{1,0:T(8,128)}, u32[]{:S(2)}) copy-start(s32[8,4]{1,0:T(8,128)} %copy-done.15) | copy-start | bytes 388 | tf_op jit(solution)/shard_map/while
  475.4 7.7 %copy-start.8 = (bf16[8,128,768]{2,1,0:T(8,128)(2,1)S(1)}, bf16[8,128,768]{2,1,0:T(8,128)(2,1)}, u32[]{:S(2)}) copy-start(bf16[8,128,768]{2,1,0:T(8,128)(2,1)} %get-tuple-element.400) | copy-start | bytes 4718596
  475.4 7.7 %copy-start.10 = (bf16[1024,768]{1,0:T(8,128)(2,1)S(1)}, bf16[1024,768]{1,0:T(8,128)(2,1)}, u32[]{:S(2)}) copy-start(bf16[1024,768]{1,0:T(8,128)(2,1)} %param.36) | copy-start | bytes 4718596
  477.2 12.2 %collective-permute-start = (bf16[128,768]{1,0:T(8,128)(2,1)S(1)}, bf16[128,768]{1,0:T(8,128)(2,1)S(1)}, u32[]{:S(2)}, u32[]{:S(2)}) collective-permute-start(bf16[128,768]{1,0:T(8,128)(2,1)S(1)} %get-tuple-element.209), channel_id=1, source_target_pairs={{0,1},{1,2},{2,3},{3,4},{4,5},{5,6},{6,7},{7,8},{8,9},{9,10},{10,1... | collective-permute-start | bytes 589832 | tf_op jit(solution)/shard_map/ppermute | solution.py:49
  477.5 12.0 %collective-permute-start.1 = (bf16[128,768]{1,0:T(8,128)(2,1)S(1)}, bf16[128,768]{1,0:T(8,128)(2,1)S(1)}, u32[]{:S(2)}, u32[]{:S(2)}) collective-permute-start(bf16[128,768]{1,0:T(8,128)(2,1)S(1)} %get-tuple-element.208), channel_id=1, source_target_pairs={{0,2},{1,3},{2,4},{3,5},{4,6},{5,7},{6,8},{7,9},{8,10},{9,11},{10,... | collective-permute-start | bytes 589832 | tf_op jit(solution)/shard_map/ppermute | solution.py:49
  479.3 11.7 %collective-permute-start.2 = (bf16[128,768]{1,0:T(8,128)(2,1)S(1)}, bf16[128,768]{1,0:T(8,128)(2,1)S(1)}, u32[]{:S(2)}, u32[]{:S(2)}) collective-permute-start(bf16[128,768]{1,0:T(8,128)(2,1)S(1)} %get-tuple-element.207), channel_id=1, source_target_pairs={{0,3},{1,4},{2,5},{3,6},{4,7},{5,8},{6,9},{7,10},{8,11},{9,12},{10... | collective-permute-start | bytes 589832 | tf_op jit(solution)/shard_map/ppermute | solution.py:49
  480.3 32.5 %collective-permute-start.3 = (bf16[128,768]{1,0:T(8,128)(2,1)S(1)}, bf16[128,768]{1,0:T(8,128)(2,1)S(1)}, u32[]{:S(2)}, u32[]{:S(2)}) collective-permute-start(bf16[128,768]{1,0:T(8,128)(2,1)S(1)} %get-tuple-element.206), channel_id=1, source_target_pairs={{0,4},{1,5},{2,6},{3,7},{4,8},{5,9},{6,10},{7,11},{8,12},{9,13},{1... | collective-permute-start | bytes 589832 | tf_op jit(solution)/shard_map/ppermute | solution.py:49
  480.4 37.4 %copy-start.12 = (s32[1024]{0:T(1024)S(1)}, s32[1024]{0:T(1024)}, u32[]{:S(2)}) copy-start(s32[1024]{0:T(1024)} %copy-done.11) | copy-start | bytes 12292
  480.4 37.4 %copy-start.14 = (s32[1024]{0:T(1024)S(1)}, s32[1024]{0:T(1024)}, u32[]{:S(2)}) copy-start(s32[1024]{0:T(1024)} %get-tuple-element.236) | copy-start | bytes 12292
  480.4 32.5 %collective-permute-start.4 = (bf16[128,768]{1,0:T(8,128)(2,1)S(1)}, bf16[128,768]{1,0:T(8,128)(2,1)S(1)}, u32[]{:S(2)}, u32[]{:S(2)}) collective-permute-start(bf16[128,768]{1,0:T(8,128)(2,1)S(1)} %get-tuple-element.205), channel_id=1, source_target_pairs={{0,5},{1,6},{2,7},{3,8},{4,9},{5,10},{6,11},{7,12},{8,13},{9,14},{... | collective-permute-start | bytes 589832 | tf_op jit(solution)/shard_map/ppermute | solution.py:49
  489.4 23.5 %collective-permute-start.5 = (bf16[128,768]{1,0:T(8,128)(2,1)S(1)}, bf16[128,768]{1,0:T(8,128)(2,1)S(1)}, u32[]{:S(2)}, u32[]{:S(2)}) collective-permute-start(bf16[128,768]{1,0:T(8,128)(2,1)S(1)} %get-tuple-element.204), channel_id=1, source_target_pairs={{0,6},{1,7},{2,8},{3,9},{4,10},{5,11},{6,12},{7,13},{8,14},{9,15},... | collective-permute-start | bytes 589832 | tf_op jit(solution)/shard_map/ppermute | solution.py:49
  489.4 23.5 %collective-permute-start.6 = (bf16[128,768]{1,0:T(8,128)(2,1)S(1)}, bf16[128,768]{1,0:T(8,128)(2,1)S(1)}, u32[]{:S(2)}, u32[]{:S(2)}) collective-permute-start(bf16[128,768]{1,0:T(8,128)(2,1)S(1)} %get-tuple-element.203), channel_id=1, source_target_pairs={{0,7},{1,8},{2,9},{3,10},{4,11},{5,12},{6,13},{7,14},{8,15},{9,0},... | collective-permute-start | bytes 589832 | tf_op jit(solution)/shard_map/ppermute | solution.py:49
  490.9 26.9 %collective-permute-start.7 = (bf16[128,768]{1,0:T(8,128)(2,1)S(1)}, bf16[128,768]{1,0:T(8,128)(2,1)S(1)}, u32[]{:S(2)}, u32[]{:S(2)}) collective-permute-start(bf16[128,768]{1,0:T(8,128)(2,1)S(1)} %get-tuple-element.202), channel_id=1, source_target_pairs={{0,8},{1,9},{2,10},{3,11},{4,12},{5,13},{6,14},{7,15},{8,0},{9,1},... | collective-permute-start | bytes 589832 | tf_op jit(solution)/shard_map/ppermute | solution.py:49
  517.8 32.8 %copy-start.1 = (s32[16,8]{0,1:T(8,128)S(1)}, s32[16,8]{0,1:T(8,128)}, u32[]{:S(2)}) copy-start(s32[16,8]{0,1:T(8,128)} %param.27) | copy-start | bytes 1540
  (30 other events, 102.9 us)
where the time goes:
time: 557 us; the launch traced here: 552 us
  local copies, waits for them, and re-layouts  168 us (30%)
  matrix products  145 us (26%)
  blocking collectives  91.6 us (16%)
  waiting for transfers between devices  67.1 us (12%)
  other arithmetic  30.3 us (5%)
  loops' own time  20 us (4%)
  between operations  17.7 us (3%)
  starting transfers between devices  12.1 us (2%)
    all_to_all x1, blocking collectives, cut_exchange(): lax.all_to_all(piece, axis, split_axis=0, concat_axis=0, tiled=True)  63.6 us
    gather x8, local copies, waits for them, and re-layouts, attend(): w_value[src_types]  39.7 us
    all_to_all x1, waiting for transfers between devices, cut_exchange(): lax.all_to_all(piece, axis, split_axis=0, concat_axis=0, tiled=True)  34.6 us
    ppermute x8, waiting for transfers between devices, shifted(): lax.ppermute(array, axis, [(i, (i + by) % count) for i in range(count)])  32.4 us
    dot_general x8, matrix products, attend(): jnp.einsum('hin,nhe->ihe', attention, message.reshape(NT * TILE, HEADS, D...  30.9 us
    psum x4, blocking collectives, over_axes(): array = lax.psum(array, axis)  28 us
    dot_general x8, matrix products, attend(): jnp.einsum('jmd,jde->jme', src_tiles, w_value[src_types], preferred_eleme...  27.6 us
    dot_general x8, matrix products, attend(): jnp.einsum('jmd,jde->jme', src_tiles, w_key[src_types], preferred_element...  27.6 us
  transfers between devices with their start and end apart: 9, of which 5 were waited for; matrix products, arithmetic and copies ran while one was open for 3% of the time, Pallas kernels for 0%

commit v1 on v0

v1 whole, which is shorter than its diff:
```python
import functools
import math

import jax
import jax.numpy as jnp
from jax import lax
from jax.experimental import pallas as pl
from jax.experimental.pallas import tpu as pltpu
from jax.sharding import Mesh
from jax.sharding import PartitionSpec as P

D = 768
HEADS = 8
DH = 96
TILE = 128
HALF = TILE // 2
NT = 4
NB = 8
REQ = NB * NT
RING = 4
CAP = 3
NREL = 5
STEPS = 8
LANES = 16
WIN = 256
WINDOW = [0, 0, 128, 256, 256, 384, 512, 512]
STRIP = [(0, 384), (128, 640), (384, 768)]
DOM_NARROW = ("dom_0", "dom_1", "narrow_0", "narrow_1")
DOM = ("dom_0", "dom_1")
MESH = pl.DeviceIdType.MESH
BF = jnp.bfloat16
F32 = jnp.float32

SEL = 0
IDX = 72
STYPE = 136
RELA = 168
OTYPE = 200
SCHED = 208
NTYP = 216
TABLE = 224


def prep_kernel(tiles, types, relation, sched, out, count):
    z = lax.axis_index("narrow_0")
    x = lax.axis_index("narrow_1")
    lane = z * RING + x

    def clear(i, c):
        out[SEL + i] = 0
        return c

    lax.fori_loop(0, 72, clear, 0)

    def scan(dst, visit):
        def zero(i, c):
            count[i] = 0
            return c

        lax.fori_loop(0, LANES, zero, 0)

        def body(p, c):
            t = tiles[dst * REQ + p]
            owner = t // NB
            k = count[owner]
            count[owner] = k + 1
            visit(p, t, owner, t % NB, k)
            return c

        lax.fori_loop(0, REQ, body, 0)

    def mine(p, t, owner, blk, k):
        oz = (z - owner // RING) % RING
        ox = (x - owner % RING) % RING
        out[IDX + p] = jnp.where(
            oz == 0, ox * NB + blk, 32 + (oz - 1) * 12 + ox * CAP + k
        )
        out[IDX + REQ + p] = jnp.where(
            ox == 0, oz * NB + blk, 32 + (ox - 1) * 12 + oz * CAP + k
        )
        out[STYPE + p] = types[t]
        out[RELA + p] = relation[p]

    scan(lane, mine)
    for d in range(1, RING):

        def row(p, t, owner, blk, k, d=d):
            @pl.when(owner // RING == z)
            def _():
                out[SEL + (d - 1) * 12 + (x - owner % RING) % RING * CAP + k] = blk

        scan((z + d) % RING * RING + x, row)

        def col(p, t, owner, blk, k, d=d):
            @pl.when(owner % RING == x)
            def _():
                out[SEL + 36 + (d - 1) * 12 + (z - owner // RING) % RING * CAP + k] = blk

        scan(z * RING + (x + d) % RING, col)
    for b in range(NB):
        out[OTYPE + b] = types[lane * NB + b]
    for s in range(STEPS):
        out[SCHED + s] = sched[lane * STEPS + s]
        frm = (lane - s - 1 + LANES) % LANES
        out[NTYP + s] = types[frm * NB + sched[frm * STEPS + s]]


def prep(tiles, types, relation, sched):
    smem = pl.BlockSpec(memory_space=pltpu.SMEM)
    return pl.pallas_call(
        prep_kernel,
        name="prep",
        out_shape=jax.ShapeDtypeStruct((TABLE,), jnp.int32),
        in_specs=[smem] * 4,
        out_specs=smem,
        scratch_shapes=[pltpu.SMEM((LANES,), jnp.int32)],
    )(tiles.reshape(-1), types, relation.reshape(-1), sched.reshape(-1))


def exchange_kernel(tab, feats, out, held, near, far, send, transit, lsem, s1, r1, s2, r2):
    coord = [lax.axis_index("narrow_1"), lax.axis_index("narrow_0")]
    name = ["narrow_1", "narrow_0"]

    def to(axis, by):
        return {name[axis]: (coord[axis] + by) % RING}

    local = [
        pltpu.make_async_copy(
            feats.at[:, pl.ds(rt * HALF, HALF), :], near.at[rt, pl.ds(0, NB)], lsem.at[rt]
        )
        for rt in range(2)
    ]
    for c in local:
        c.start()
    barrier = pltpu.get_barrier_semaphore()
    for axis in range(2):
        for by in (1, 3):
            pl.semaphore_signal(barrier, 1, device_id=to(axis, by), device_id_type=MESH)
    pl.semaphore_wait(barrier, 4)
    for c in local:
        c.wait()

    def first(rt, way, part):
        by = slot = (1, 3)[way]
        half = part if way == 0 else 1 - part
        return pltpu.make_async_remote_copy(
            src_ref=near.at[rt, pl.ds(half * 4, 4)],
            dst_ref=near.at[rt, pl.ds(slot * NB + half * 4, 4)],
            send_sem=s1.at[rt, way, part],
            recv_sem=r1.at[rt, way, part],
            device_id=to(rt, by),
            device_id_type=MESH,
        )

    def forward(rt, way):
        by = slot = (1, 3)[way]
        return pltpu.make_async_remote_copy(
            src_ref=near.at[rt, pl.ds(slot * NB + way * 4, 4)],
            dst_ref=near.at[rt, pl.ds(2 * NB + way * 4, 4)],
            send_sem=s1.at[rt, way, 2],
            recv_sem=r1.at[rt, way, 2],
            device_id=to(rt, by),
            device_id_type=MESH,
        )

    def second(rt, d, o):
        at = pl.ds((d - 1) * 12 + o * CAP, CAP)
        if d == 2:
            dst = transit.at[rt, pl.ds(o * CAP, CAP)]
            by = 1 if o < 2 else 3
        else:
            dst = far.at[rt, at]
            by = d
        return pltpu.make_async_remote_copy(
            src_ref=send.at[rt, at],
            dst_ref=dst,
            send_sem=s2.at[rt, d - 1, o],
            recv_sem=r2.at[rt, d - 1, o],
            device_id=to(1 - rt, by),
            device_id_type=MESH,
        )

    def onward(rt, o):
        return pltpu.make_async_remote_copy(
            src_ref=transit.at[rt, pl.ds(o * CAP, CAP)],
            dst_ref=far.at[rt, pl.ds(12 + o * CAP, CAP)],
            send_sem=s2.at[rt, 3, o],
            recv_sem=r2.at[rt, 3, o],
            device_id=to(1 - rt, 1 if o < 2 else 3),
            device_id_type=MESH,
        )

    def keep(rt, o):
        held[rt, o * NB : (o + 1) * NB] = near[rt, o * NB : (o + 1) * NB]

    def keep_far(rt, d, o):
        at = (d - 1) * 12 + o * CAP
        held[rt, 32 + at : 32 + at + CAP] = far[rt, at : at + CAP]

    def pick(rt, o):
        for d in (2, 1, 3):
            for k in range(CAP):
                at = (d - 1) * 12 + o * CAP + k
                blk = tab[SEL + rt * 36 + at]
                send[rt, at] = held[rt, o * NB + blk]
            second(rt, d, o).start()

    for part in range(2):
        for rt in range(2):
            for way in range(2):
                first(rt, way, part).start()
    for rt in range(2):
        keep(rt, 0)
        pick(rt, 0)
    for rt in range(2):
        for way in range(2):
            first(rt, way, 0).wait_recv()
            forward(rt, way).start()
    for rt in range(2):
        second(rt, 2, 0).wait_recv()
        onward(rt, 0).start()
    for o, way in ((1, 0), (3, 1)):
        for rt in range(2):
            first(rt, way, 1).wait_recv()
            keep(rt, o)
            pick(rt, o)
    for rt in range(2):
        for way in range(2):
            forward(rt, way).wait_recv()
        keep(rt, 2)
        pick(rt, 2)
    for o in (1, 3, 2):
        for rt in range(2):
            second(rt, 2, o).wait_recv()
            onward(rt, o).start()
    for o in (0, 1, 3, 2):
        for rt in range(2):
            for d in (1, 3):
                second(rt, d, o).wait_recv()
                keep_far(rt, d, o)
            onward(rt, o).wait_recv()
            keep_far(rt, 2, o)

    def collect(p, c):
        out[p, 0:HALF, :] = held[0, tab[IDX + p]]
        out[p, HALF:TILE, :] = held[1, tab[IDX + REQ + p]]
        return c

    lax.fori_loop(0, REQ, collect, 0)
    for rt in range(2):
        for way in range(2):
            for part in range(2):
                first(rt, way, part).wait_send()
            forward(rt, way).wait_send()
        for o in range(4):
            for d in (1, 2, 3):
                second(rt, d, o).wait_send()
            onward(rt, o).wait_send()


def exchange(table, feats):
    return pl.pallas_call(
        exchange_kernel,
        name="exchange",
        out_shape=jax.ShapeDtypeStruct((REQ, TILE, D), BF),
        in_specs=[
            pl.BlockSpec(memory_space=pltpu.SMEM),
            pl.BlockSpec(memory_space=pl.ANY),
        ],
        out_specs=pl.BlockSpec(memory_space=pltpu.VMEM),
        scratch_shapes=[
            pltpu.VMEM((2, 68, HALF, D), BF),
            pltpu.VMEM((2, 32, HALF, D), BF),
            pltpu.VMEM((2, 36, HALF, D), BF),
            pltpu.VMEM((2, 36, HALF, D), BF),
            pltpu.VMEM((2, 12, HALF, D), BF),
            pltpu.SemaphoreType.DMA((2,)),
            pltpu.SemaphoreType.DMA((2, 2, 3)),
            pltpu.SemaphoreType.DMA((2, 2, 3)),
            pltpu.SemaphoreType.DMA((2, 4, 4)),
            pltpu.SemaphoreType.DMA((2, 4, 4)),
        ],
        compiler_params=pltpu.CompilerParams(
            collective_id=0, has_side_effects=True, vmem_limit_bytes=60 << 20
        ),
    )(table, feats)


def dot(a, b):
    return jnp.dot(a, b, preferred_element_type=F32)


def dot_t(a, b):
    return lax.dot_general(a, b, (((1,), (1,)), ((), ())), preferred_element_type=F32)


STRIP_AT = [0, 384, 896]
STRIPS = 1280


def head_of(index):
    return sum((index >= DH * h).astype(jnp.int32) for h in range(1, HEADS))


def widen(rel, wide):
    for c, (lo, hi) in enumerate(STRIP):
        col = lax.broadcasted_iota(jnp.int32, (DH, WIN), 1) + c * WIN
        row = lax.broadcasted_iota(jnp.int32, (DH, WIN), 0)
        place = (col - DH * head_of(col) == row).astype(F32).astype(BF)
        full = dot(rel[lo:hi, :], place)
        col = lax.broadcasted_iota(jnp.int32, (hi - lo, WIN), 1) + c * WIN
        row = lax.broadcasted_iota(jnp.int32, (hi - lo, WIN), 0) + lo
        full = jnp.where(head_of(row) == head_of(col), full, 0.0)
        wide[STRIP_AT[c] : STRIP_AT[c] + hi - lo, :] = full.astype(BF)


def spread(rows, wide):
    return jnp.concatenate(
        [
            dot(rows[:, lo:hi], wide[STRIP_AT[c] : STRIP_AT[c] + hi - lo, :])
            for c, (lo, hi) in enumerate(STRIP)
        ],
        axis=1,
    ).astype(BF)


def attend_kernel(
    tab, prior, gate, blocks, fetched, wq, wk, wv, wo, att, msg, out,
    keyed, message, agg, att_wide, msg_wide
):
    b = pl.program_id(0)

    @pl.when(b == 0)
    def _():
        def body(r, c):
            widen(att.at[r], att_wide.at[r])
            widen(msg.at[r], msg_wide.at[r])
            return c

        lax.fori_loop(0, NREL, body, 0)

    tb = tab[OTYPE + b]
    rows = blocks[0]
    query = dot(rows, wq[tb]).astype(BF)
    for j in range(NT):
        ts = tab[STYPE + b * NT + j]
        r = tab[RELA + b * NT + j]
        src = fetched[j]
        key = dot(src, wk[ts]).astype(BF)
        value = dot(src, wv[ts]).astype(BF)
        at = pl.ds(j * TILE, TILE)
        keyed[at, :] = spread(key, att_wide.at[r])
        message[at, :] = spread(value, msg_wide.at[r])
    agg[...] = jnp.zeros_like(agg)
    column = lax.broadcasted_iota(jnp.int32, (TILE, WIN), 1)
    for h in range(HEADS):
        w = WINDOW[h]
        lo = h * DH - w
        mine = (column >= lo) & (column < lo + DH)
        q = jnp.where(mine, query[:, w : w + WIN].astype(F32), 0.0).astype(BF)
        scores = []
        for j in range(NT):
            scale = prior[tab[RELA + b * NT + j] * HEADS + h] * (1.0 / math.sqrt(DH))
            s = dot_t(q, keyed[j * TILE : (j + 1) * TILE, w : w + WIN])
            scores.append(s * scale)
        top = jnp.maximum(jnp.maximum(scores[0], scores[1]), jnp.maximum(scores[2], scores[3]))
        top = jnp.max(top, axis=1, keepdims=True)
        weights = [jnp.exp(s - top) for s in scores]
        total = jnp.sum((weights[0] + weights[1]) + (weights[2] + weights[3]), axis=1, keepdims=True)
        inv = 1.0 / total
        attention = jnp.concatenate([(e * inv).astype(BF) for e in weights], axis=1)
        got = dot(attention, message[:, w : w + WIN])
        agg[:, w : w + WIN] += jnp.where(mine, got, 0.0)
    merged = agg[...]
    active = (0.5 * merged * (1.0 + lax.erf(merged * math.sqrt(0.5)))).astype(BF)
    projected = dot(active, wo[tb])
    a = jax.nn.sigmoid(jnp.full((1, D), gate[tb], F32))
    out[0] = (a * projected + (1.0 - a) * rows.astype(F32)).astype(BF)


def attend(table, prior, gate, blocks, fetched, wq, wk, wv, wo, att, msg):
    def whole(shape):
        return pl.BlockSpec(
            shape, lambda b, *_: (0,) * len(shape), pipeline_mode=pl.Buffered(1)
        )

    weight = whole((3, D, D))
    wide = whole((NREL, D, DH))
    return pl.pallas_call(
        attend_kernel,
        name="attend",
        out_shape=jax.ShapeDtypeStruct((NB, TILE, D), BF),
        grid_spec=pltpu.PrefetchScalarGridSpec(
            num_scalar_prefetch=3,
            grid=(NB,),
            in_specs=[
                pl.BlockSpec((1, TILE, D), lambda b, *_: (b, 0, 0)),
                pl.BlockSpec((NT, TILE, D), lambda b, *_: (b, 0, 0)),
                weight,
                weight,
                weight,
                weight,
                wide,
                wide,
            ],
            out_specs=pl.BlockSpec((1, TILE, D), lambda b, *_: (b, 0, 0)),
            scratch_shapes=[
                pltpu.VMEM((NT * TILE, D), BF),
                pltpu.VMEM((NT * TILE, D), BF),
                pltpu.VMEM((TILE, D), F32),
                pltpu.VMEM((NREL, STRIPS, WIN), BF),
                pltpu.VMEM((NREL, STRIPS, WIN), BF),
            ],
        ),
        compiler_params=pltpu.CompilerParams(vmem_limit_bytes=60 << 20),
    )(table, prior, gate, blocks, fetched, wq, wk, wv, wo, att, msg)


def contrast_kernel(
    tab, weight, emb, pos, loss, mean, offer, negs, part, lanes, doms, ss, rs, sl, rl, sd, rd
):
    y = lax.axis_index("dom_0")
    core = lax.axis_index("dom_1")
    z = lax.axis_index("narrow_0")
    x = lax.axis_index("narrow_1")
    lane = z * RING + x
    dom = y * 2 + core

    def lane_id(by):
        other = (lane + by) % LANES
        return {"narrow_0": other // RING, "narrow_1": other % RING}

    def dom_id(by):
        other = (dom + by) % 8
        return {"dom_0": other // 2, "dom_1": other % 2}

    barrier = pltpu.get_barrier_semaphore()
    for by in range(1, LANES):
        pl.semaphore_signal(barrier, 1, device_id=lane_id(by), device_id_type=MESH)
    for by in range(1, 8):
        pl.semaphore_signal(barrier, 1, device_id=dom_id(by), device_id_type=MESH)
    pl.semaphore_wait(barrier, LANES - 1 + 7)

    def give(s):
        return pltpu.make_async_remote_copy(
            src_ref=offer.at[s],
            dst_ref=negs.at[s],
            send_sem=ss.at[s],
            recv_sem=rs.at[s],
            device_id=lane_id(s + 1),
            device_id_type=MESH,
        )

    for s in range(STEPS):
        offer[s] = emb[tab[SCHED + s]]
        give(s).start()
    for s in range(STEPS):
        give(s).wait_recv()

    inv = 1.0 / math.sqrt(D)
    total = jnp.zeros((1, TILE), F32)
    for b in range(NB):
        own = emb[b]
        tb = tab[OTYPE + b]
        prod = own.astype(F32) * pos[b].astype(F32)
        fold = prod[:, 0:TILE]
        for c in range(1, D // TILE):
            fold = fold + prod[:, c * TILE : (c + 1) * TILE]
        positive = jnp.sum(fold.T, axis=0, keepdims=True) * inv
        logits = []
        high = positive
        for s in range(STEPS):
            v = dot_t(negs[s], own) * inv
            v = jnp.where(tab[NTYP + s] == tb, v, -jnp.inf)
            high = jnp.maximum(high, jnp.max(v, axis=0, keepdims=True))
            logits.append(v)
        den = jnp.exp(positive - high)
        for v in logits:
            den = den + jnp.sum(jnp.exp(v - high), axis=0, keepdims=True)
        row = high + jnp.log(den) - positive
        loss[b : b + 1, :] = row
        total = total + row * weight[tb]
    part[...] = jnp.broadcast_to(total, (8, TILE))

    def lane_copy(by):
        return pltpu.make_async_remote_copy(
            src_ref=part,
            dst_ref=lanes.at[by],
            send_sem=sl.at[by],
            recv_sem=rl.at[by],
            device_id=lane_id(by),
            device_id_type=MESH,
        )

    for by in range(1, LANES):
        lane_copy(by).start()
    lanes[0] = part[...]
    for by in range(1, LANES):
        lane_copy(by).wait_recv()
    for by in range(1, LANES):
        lane_copy(by).wait_send()
    acc = lanes[lane]
    for a in range(1, LANES):
        acc = acc + lanes[(lane - a + LANES) % LANES]
    doms[0] = acc

    def dom_copy(by):
        return pltpu.make_async_remote_copy(
            src_ref=doms.at[0],
            dst_ref=doms.at[by],
            send_sem=sd.at[by],
            recv_sem=rd.at[by],
            device_id=dom_id(by),
            device_id_type=MESH,
        )

    for by in range(1, 8):
        dom_copy(by).start()
    for by in range(1, 8):
        dom_copy(by).wait_recv()
    acc = doms[dom]
    for a in range(1, 8):
        acc = acc + doms[(dom - a + 8) % 8]
    whole = jnp.sum(acc, axis=1, keepdims=True) * (1.0 / (NB * TILE * 128))
    mean[...] = jnp.broadcast_to(whole, (8, TILE))
    for by in range(1, 8):
        dom_copy(by).wait_send()
    for s in range(STEPS):
        give(s).wait_send()


def contrast(table, weight, emb, pos):
    smem = pl.BlockSpec(memory_space=pltpu.SMEM)
    vmem = pl.BlockSpec(memory_space=pltpu.VMEM)
    return pl.pallas_call(
        contrast_kernel,
        name="contrast",
        out_shape=(
            jax.ShapeDtypeStruct((NB, TILE), F32),
            jax.ShapeDtypeStruct((8, TILE), F32),
        ),
        in_specs=[smem, smem, vmem, vmem],
        out_specs=(vmem, vmem),
        scratch_shapes=[
            pltpu.VMEM((STEPS, TILE, D), BF),
            pltpu.VMEM((STEPS, TILE, D), BF),
            pltpu.VMEM((8, TILE), F32),
            pltpu.VMEM((LANES, 8, TILE), F32),
            pltpu.VMEM((8, 8, TILE), F32),
            pltpu.SemaphoreType.DMA((STEPS,)),
            pltpu.SemaphoreType.DMA((STEPS,)),
            pltpu.SemaphoreType.DMA((LANES,)),
            pltpu.SemaphoreType.DMA((LANES,)),
            pltpu.SemaphoreType.DMA((8,)),
            pltpu.SemaphoreType.DMA((8,)),
        ],
        compiler_params=pltpu.CompilerParams(
            collective_id=1, has_side_effects=True, vmem_limit_bytes=60 << 20
        ),
    )(table, weight, emb, pos)


def shards(
    feats,
    node_type,
    tiles,
    relation,
    neg_sched,
    w_query,
    w_key,
    w_value,
    w_out,
    rel_att,
    rel_msg,
    rel_prior,
    skip_gate,
    pos_view,
    type_weight,
):
    table = prep(tiles, node_type, relation, neg_sched)
    blocks = feats.reshape(NB, TILE, D)
    fetched = exchange(table, blocks)
    emb = attend(
        table,
        rel_prior.reshape(-1),
        skip_gate,
        blocks,
        fetched,
        w_query,
        w_key,
        w_value,
        w_out,
        rel_att.reshape(NREL, D, DH),
        rel_msg.reshape(NREL, D, DH),
    )
    loss, mean = contrast(table, type_weight, emb, pos_view.reshape(NB, TILE, D))
    return emb.reshape(NB * TILE, D), loss.reshape(NB * TILE), mean[0, 0]


def solution(mesh):
    finer = Mesh(mesh.devices.reshape(4, 2, 4, 4), DOM_NARROW)
    in_specs = (
        P(DOM_NARROW, None),
        P(DOM),
        P(DOM, None),
        P(DOM_NARROW, None),
        P(DOM, None),
        P(),
        P(),
        P(),
        P(),
        P(),
        P(),
        P(),
        P(),
        P(DOM_NARROW, None),
        P(),
    )
    out_specs = (P(DOM_NARROW, None), P(DOM_NARROW), P())
    return jax.shard_map(
        shards, mesh=finer, in_specs=in_specs, out_specs=out_specs, check_vma=False
    )
```

time: 557 us -> 215 us (0.39)
  Pallas kernels: 0 us -> 206 us
  local copies, waits for them, and re-layouts: 168 us -> 7.96 us
  matrix products: 145 us -> 0 us
  blocking collectives: 91.6 us -> 0 us
  waiting for transfers between devices: 67.1 us -> 0 us
  other arithmetic: 30.3 us -> 0 us
  loops' own time: 20 us -> 0 us
  between operations: 17.7 us -> 0.66 us
  starting transfers between devices: 12.1 us -> 0 us
    pallas_call x0 -> x4, Pallas kernels: none -> 206 us  [the longest x1 88.2 us: exchange(): pl.pallas_call(exchange_kernel, name='exchange', out_shape=jax.ShapeDtype...]
    dot_general x57 -> x0, matrix products: 145 us -> none  [the longest x8 30.9 us: attend(): jnp.einsum('hin,nhe->ihe', attention, message.reshape(NT * TILE, HEADS, D...]
    gather x47 -> x0, local copies, waits for them, and re-layouts: 105 us -> none  [the longest x8 39.7 us: attend(): w_value[src_types]]
    all_to_all x1 -> x0, blocking collectives: 63.6 us -> none  [cut_exchange(): lax.all_to_all(piece, axis, split_axis=0, concat_axis=0, tiled=True)]
    all_to_all x1 -> x0, waiting for transfers between devices: 34.6 us -> none  [cut_exchange(): lax.all_to_all(piece, axis, split_axis=0, concat_axis=0, tiled=True)]
    ppermute x8 -> x0, waiting for transfers between devices: 32.4 us -> none  [shifted(): lax.ppermute(array, axis, [(i, (i + by) % count) for i in range(count)])]
    psum x4 -> x0, blocking collectives: 28 us -> none  [over_axes(): array = lax.psum(array, axis)]
    another operation x1 -> x0, loops' own time: 20 us -> none  [shards(): lax.map(attend, (blocks, own_types, fetched, source_types, relation))]
  transfers between devices with their start and end apart: 9 -> 0, of which waited for: 5 -> 0; matrix products, arithmetic and copies ran while one was open for 3% -> 0% of each run, Pallas kernels for 0% -> 0%
where the time goes in v1:
time: 215 us
  Pallas kernels  206 us (96%)
  local copies, waits for them, and re-layouts  7.96 us (4%)
    pallas_call x1, Pallas kernels, exchange(): pl.pallas_call(exchange_kernel, name='exchange', out_shape=jax.ShapeDtype...  88.2 us
    pallas_call x1, Pallas kernels, contrast(): pl.pallas_call(contrast_kernel, name='contrast', out_shape=(jax.ShapeDtyp...  55 us
    pallas_call x1, Pallas kernels, attend(): pl.pallas_call(attend_kernel, name='attend', out_shape=jax.ShapeDtypeStru...  54.9 us
    pallas_call x1, Pallas kernels, prep(): pl.pallas_call(prep_kernel, name='prep', out_shape=jax.ShapeDtypeStruct((...  8.22 us

profile of v1, /device:TPU:1, one launch (start us, length us, event | category | flops | bytes accessed | tf_op | source)
XLA Modules:
  0.0 215.0 jit_solution(17723008418276850397)
XLA Ops:
  0.6 1.3 reshape.39.prior
  2.0 0.8 copy.21
  2.7 0.6 reshape.37.relation
  3.3 0.8 copy.22
  4.1 0.6 reshape.38.sched
  4.7 0.8 copy.20
  5.5 0.7 reshape.36.tiles
  6.2 8.2 %prep.1.tab = s32[224]{0:T(256)} custom-call(s32[512]{0:T(512)} %reshape.36.tiles, s32[128]{0:T(128)} %types.1, s32[32]{0:T(128)} %reshape.37.relation, s32[128]{0:T(128)} %reshape.38.sched), custom_call_target="tpu_custom_call" | custom-call | tf_op jit(solution)/shard_map/prep/pallas_call | solution.py:110
  14.4 88.2 %exchange.1.fetched = bf16[32,128,768]{2,1,0:T(8,128)(2,1)} custom-call(s32[224]{0:T(256)} %prep.1.tab, bf16[8,128,768]{2,1,0:T(8,128)(2,1)} %bitcast.7), custom_call_target="tpu_custom_call" | custom-call | tf_op jit(solution)/shard_map/exchange/pallas_call | solution.py:262
  102.6 54.9 %attend.1.emb = bf16[8,128,768]{2,1,0:T(8,128)(2,1)} custom-call(s32[224]{0:T(256)} %prep.1.tab, f32[40]{0:T(128)} %reshape.39.prior, f32[3]{0:T(128)} %gate.1, bf16[8,128,768]{2,1,0:T(8,128)(2,1)} %bitcast.8, bf16[32,128,768]{2,1,0:T(8,128)(2,1)} %exchange.1.fetched, bf16[3,768,768]{2,1,0:T(8,128)(2,1)} %wq.1, bf16[3,768,768]{2,1,0:T(8,128)(2,1)} %wk.1, ...), custom_call_target="tpu_custom_call" | custom-call | tf_op jit(solution)/shard_map/attend/pallas_call | solution.py:389
  157.5 55.0 %contrast.1 = (f32[8,128]{1,0:T(8,128)}, f32[8,128]{1,0:T(8,128)}) custom-call(s32[224]{0:T(256)} %prep.1.tab, f32[3]{0:T(128)} %weight.1, bf16[8,128,768]{2,1,0:T(8,128)(2,1)} %attend.1.emb, bf16[8,128,768]{2,1,0:T(8,128)(2,1)} %bitcast.10), custom_call_target="tpu_custom_call" | custom-call | tf_op jit(solution)/shard_map/contrast/pallas_call | solution.py:535
  212.5 1.2 slice.3
  213.7 1.3 copy.24

commit v2 on v1

v2 whole, which is shorter than its diff:
```python
import functools
import math

import jax
import jax.numpy as jnp
from jax import lax
from jax.experimental import pallas as pl
from jax.experimental.pallas import tpu as pltpu
from jax.sharding import Mesh
from jax.sharding import PartitionSpec as P

D = 768
HEADS = 8
DH = 96
TILE = 128
HALF = TILE // 2
NT = 4
NB = 8
REQ = NB * NT
RING = 4
CAP = 3
NREL = 5
STEPS = 8
LANES = 16
WIN = 256
STRIP = [(0, 384), (128, 640), (384, 768)]
DOM_NARROW = ("dom_0", "dom_1", "narrow_0", "narrow_1")
DOM = ("dom_0", "dom_1")
MESH = pl.DeviceIdType.MESH
BF = jnp.bfloat16
F32 = jnp.float32

SEL = 0
IDX = 72
STYPE = 136
RELA = 168
PLACE = 200
ORDER = 232
STAGE = 264
OTYPE = 296
TABLE = 304
READY = [11, 17, 23, 32]
STAGE_OF = {(1, 3): 1, (3, 1): 1, (2, 3): 2, (3, 2): 2, (1, 2): 3, (2, 1): 3, (2, 2): 3}
STRIP_AT = [0, 384, 896]
STRIPS = 1280
PAIR = [0, 128, 384, 512]


def dot(a, b):
    return jnp.dot(a, b, preferred_element_type=F32)


def dot_t(a, b):
    return lax.dot_general(a, b, (((1,), (1,)), ((), ())), preferred_element_type=F32)


def head_of(index):
    return sum((index >= DH * h).astype(jnp.int32) for h in range(1, HEADS))


def widen(rel, wide):
    for c, (lo, hi) in enumerate(STRIP):
        col = lax.broadcasted_iota(jnp.int32, (DH, WIN), 1) + c * WIN
        row = lax.broadcasted_iota(jnp.int32, (DH, WIN), 0)
        place = (col - DH * head_of(col) == row).astype(F32).astype(BF)
        full = dot(rel[lo:hi, :], place)
        col = lax.broadcasted_iota(jnp.int32, (hi - lo, WIN), 1) + c * WIN
        row = lax.broadcasted_iota(jnp.int32, (hi - lo, WIN), 0) + lo
        full = jnp.where(head_of(row) == head_of(col), full, 0.0)
        wide[STRIP_AT[c] : STRIP_AT[c] + hi - lo, :] = full.astype(BF)


def spread(rows, wide):
    return jnp.concatenate(
        [
            dot(rows[:, lo:hi], wide[STRIP_AT[c] : STRIP_AT[c] + hi - lo, :])
            for c, (lo, hi) in enumerate(STRIP)
        ],
        axis=1,
    )


def layer_kernel(
    tiles, types, relation, prior, gate, feats, wq, wk, wv, wo, att, msg,
    out,
    tab, near0, near1, near2, near3, far, held, send, transit,
    wqo, wks, wvs, raw, att_wide, msg_wide, turned, keyed, message, pairs, agg,
    lsem, wsem, esem, s1, r1, s2, r2,
):
    z = lax.axis_index("narrow_0")
    x = lax.axis_index("narrow_1")
    lane = z * RING + x
    coord = [x, z]
    name = ["narrow_1", "narrow_0"]
    near = [near0, near1, near2, near3]

    def to(axis, by):
        return {name[axis]: (coord[axis] + by) % RING}

    local = [
        pltpu.make_async_copy(feats.at[:, pl.ds(rt * HALF, HALF), :], near0.at[rt], lsem.at[rt])
        for rt in range(2)
    ]
    for c in local:
        c.start()
    barrier = pltpu.get_barrier_semaphore()
    for axis in range(2):
        for by in (1, 3):
            pl.semaphore_signal(barrier, 1, device_id=to(axis, by), device_id_type=MESH)
    pl.semaphore_wait(barrier, 4)
    for c in local:
        c.wait()

    def first(rt, way, part):
        by = slot = (1, 3)[way]
        half = part if way == 0 else 1 - part
        return pltpu.make_async_remote_copy(
            src_ref=near0.at[rt, pl.ds(half * 4, 4)],
            dst_ref=near[slot].at[rt, pl.ds(half * 4, 4)],
            send_sem=s1.at[rt, way, part],
            recv_sem=r1.at[rt, way, part],
            device_id=to(rt, by),
            device_id_type=MESH,
        )

    def forward(rt, way):
        by = slot = (1, 3)[way]
        return pltpu.make_async_remote_copy(
            src_ref=near[slot].at[rt, pl.ds(way * 4, 4)],
            dst_ref=near2.at[rt, pl.ds(way * 4, 4)],
            send_sem=s1.at[rt, way, 2],
            recv_sem=r1.at[rt, way, 2],
            device_id=to(rt, by),
            device_id_type=MESH,
        )

    def second(rt, d, o):
        at = pl.ds((d - 1) * 12 + o * CAP, CAP)
        if d == 2:
            dst = transit.at[rt, pl.ds(o * CAP, CAP)]
            by = 1 if o < 2 else 3
        else:
            dst = far.at[rt, at]
            by = d
        return pltpu.make_async_remote_copy(
            src_ref=send.at[rt, at],
            dst_ref=dst,
            send_sem=s2.at[rt, d - 1, o],
            recv_sem=r2.at[rt, d - 1, o],
            device_id=to(1 - rt, by),
            device_id_type=MESH,
        )

    def onward(rt, o):
        return pltpu.make_async_remote_copy(
            src_ref=transit.at[rt, pl.ds(o * CAP, CAP)],
            dst_ref=far.at[rt, pl.ds(12 + o * CAP, CAP)],
            send_sem=s2.at[rt, 3, o],
            recv_sem=r2.at[rt, 3, o],
            device_id=to(1 - rt, 1 if o < 2 else 3),
            device_id_type=MESH,
        )

    def pick(o):
        for d in (2, 1, 3):
            for rt in range(2):
                for k in range(CAP):
                    at = (d - 1) * 12 + o * CAP + k
                    send[rt, at] = near[o][rt, tab[SEL + rt * 36 + at]]
                second(rt, d, o).start()

    def take(d, o):
        at = (d - 1) * 12 + o * CAP
        for rt in range(2):
            (onward(rt, o) if d == 2 else second(rt, d, o)).wait_recv()
            held[rt, at : at + CAP] = far[rt, at : at + CAP]

    def relay(o):
        for rt in range(2):
            second(rt, 2, o).wait_recv()
            onward(rt, o).start()

    for part in range(2):
        for rt in range(2):
            for way in range(2):
                first(rt, way, part).start()
    load_wq = pltpu.make_async_copy(wq, wqo, wsem.at[0])
    load_wk = pltpu.make_async_copy(wk, wks, wsem.at[1])
    load_wv = pltpu.make_async_copy(wv, wvs, wsem.at[2])
    load_att = pltpu.make_async_copy(att, raw, wsem.at[3])
    load_msg = pltpu.make_async_copy(msg, raw, wsem.at[4])
    load_wo = pltpu.make_async_copy(wo, wqo, wsem.at[5])
    load_att.start()
    load_wq.start()
    load_wk.start()
    load_wv.start()

    for rt in range(2):
        for d in range(1, RING):
            if rt == 0:
                dst = (z + d) % RING * RING + x
            else:
                dst = z * RING + (x + d) % RING

            def ask(p, c, rt=rt, dst=dst):
                c = list(c)
                t = tiles[p % NT, dst * NB + p // NT]
                owner = t // NB
                oz = (z - owner // RING + RING) % RING
                ox = (x - owner % RING + RING) % RING
                here, o = (oz, ox) if rt == 0 else (ox, oz)
                for i in range(RING):
                    hit = jnp.logical_and(here == 0, o == i)
                    c[i] = jnp.where(hit, c[i] + c[RING + i] * (t % NB), c[i])
                    c[RING + i] = jnp.where(hit, c[RING + i] * NB, c[RING + i])
                return tuple(c)

            got = lax.fori_loop(
                0, REQ, ask, (jnp.int32(0),) * RING + (jnp.int32(1),) * RING
            )
            for o in range(RING):
                for k in range(CAP):
                    tab[SEL + rt * 36 + (d - 1) * 12 + o * CAP + k] = (
                        got[o] // NB**k
                    ) % NB
    pick(0)

    def mine(p, c):
        c = list(c)
        t = tiles[p % NT, lane * NB + p // NT]
        owner = t // NB
        oz = (z - owner // RING + RING) % RING
        ox = (x - owner % RING + RING) % RING
        back = oz * RING + ox
        k = jnp.int32(0)
        for i in range(LANES):
            hit = back == i
            k = jnp.where(hit, c[i], k)
            c[i] = jnp.where(hit, c[i] + 1, c[i])
        stage = jnp.int32(0)
        for (a, b), v in STAGE_OF.items():
            stage = jnp.where(back == a * RING + b, v, stage)
        tab[IDX + p] = jnp.where(
            oz == 0, ox * NB + t % NB, 32 + (oz - 1) * 12 + ox * CAP + k
        )
        tab[IDX + REQ + p] = jnp.where(
            ox == 0, oz * NB + t % NB, 32 + (ox - 1) * 12 + oz * CAP + k
        )
        tab[STYPE + p] = types[t]
        tab[RELA + p] = relation[p % NT, p // NT]
        tab[STAGE + p] = stage
        for v in range(3):
            c[LANES + v] = c[LANES + v] + jnp.where(stage <= v, 1, 0)
        return tuple(c)

    counts = lax.fori_loop(0, REQ, mine, (jnp.int32(0),) * (LANES + 3))[LANES:]

    def turn(p, c):
        c = list(c)
        stage = tab[STAGE + p]
        place = jnp.int32(0)
        for v in range(4):
            hit = stage == v
            place = jnp.where(hit, c[v], place)
            c[v] = jnp.where(hit, c[v] + 1, c[v])
        tab[PLACE + p] = place
        return tuple(c)

    lax.fori_loop(0, REQ, turn, (jnp.int32(0),) + tuple(counts))

    def invert(n, c):
        found = jnp.int32(0)
        for p in range(REQ):
            found = jnp.where(tab[PLACE + p] == n, p, found)
        tab[ORDER + n] = found
        return c

    lax.fori_loop(0, REQ, invert, 0)
    for b in range(NB):
        tab[OTYPE + b] = types[lane * NB + b]
    pairs[...] = jnp.zeros_like(pairs)

    def widen_all(wide):
        def body(r, c):
            widen(raw.at[r], wide.at[r])
            return c

        lax.fori_loop(0, NREL, body, 0)

    load_att.wait()
    widen_all(att_wide)
    load_msg.start()
    for rt in range(2):
        for way in range(2):
            first(rt, way, 0).wait_recv()
            forward(rt, way).start()

    load_wq.wait()

    def ask_query(b, c):
        rows = jnp.concatenate([near0[0, b], near0[1, b]], axis=0)
        turned[b] = dot(rows, wqo[tab[OTYPE + b]]).astype(BF).T
        return c

    lax.fori_loop(0, NB, ask_query, 0)
    load_wo.start()
    load_msg.wait()
    widen_all(msg_wide)
    load_wk.wait()
    load_wv.wait()
    relay(0)
    for rt in range(2):
        for way in range(2):
            first(rt, way, 1).wait_recv()
    pick(1)
    pick(3)
    for rt in range(2):
        for way in range(2):
            forward(rt, way).wait_recv()
    pick(2)

    def part_of(rt, i):
        rows = held[rt, jnp.clip(i - 32, 0, 35)]
        for o in range(RING):
            rows = jnp.where(i // NB == o, near[o][rt, jnp.clip(i - o * NB, 0, NB - 1)], rows)
        return rows

    def transform(n, c):
        p = tab[ORDER + n]
        src = jnp.concatenate(
            [part_of(0, tab[IDX + p]), part_of(1, tab[IDX + REQ + p])], axis=0
        )
        ts = tab[STYPE + p]
        r = tab[RELA + p]
        key = dot(src, wks[ts]).astype(BF)
        keyed[n] = spread(key, att_wide.at[r]).astype(BF)
        value = dot(src, wvs[ts]).astype(BF)
        message[n] = spread(value, msg_wide.at[r]).astype(BF).T
        return c

    for d, o in ((3, 0), (1, 0), (2, 0), (3, 1)):
        take(d, o)
    relay(3)
    take(3, 3)
    relay(1)
    take(1, 1)
    lax.fori_loop(0, READY[0], transform, 0)
    relay(2)
    take(1, 3)
    lax.fori_loop(READY[0], READY[1], transform, 0)
    take(3, 2)
    take(2, 3)
    lax.fori_loop(READY[1], READY[2], transform, 0)
    take(1, 2)
    take(2, 1)
    take(2, 2)
    lax.fori_loop(READY[2], READY[3], transform, 0)

    for rt in range(2):
        for way in range(2):
            for part in range(2):
                first(rt, way, part).wait_send()
            forward(rt, way).wait_send()
        for o in range(4):
            for d in (1, 2, 3):
                second(rt, d, o).wait_send()
            onward(rt, o).wait_send()
    load_wo.wait()

    left = lax.broadcasted_iota(jnp.int32, (1, WIN), 1) < TILE
    unit = math.log2(math.e) / math.sqrt(DH)

    def attend(b, c):
        where = [tab[PLACE + b * NT + j] for j in range(NT)]
        rel = [tab[RELA + b * NT + j] for j in range(NT)]
        for h in range(HEADS):
            lo = h * DH - PAIR[h // 2]
            pairs[h // 2, lo : lo + DH, h % 2 * TILE : (h % 2 + 1) * TILE] = turned[
                b, h * DH : (h + 1) * DH, :
            ]
        for q in range(HEADS // 2):
            w = PAIR[q]
            scores = []
            for j in range(NT):
                scale = jnp.where(left, prior[rel[j], 2 * q], prior[rel[j], 2 * q + 1]) * unit
                scores.append(dot(keyed[where[j], :, w : w + WIN], pairs[q]) * scale)
            top = jnp.maximum(
                jnp.maximum(scores[0], scores[1]), jnp.maximum(scores[2], scores[3])
            )
            top = jnp.max(top, axis=0, keepdims=True)
            weights = [jnp.exp2(s - top) for s in scores]
            total = jnp.sum(
                (weights[0] + weights[1]) + (weights[2] + weights[3]), axis=0, keepdims=True
            )
            inv = 1.0 / total
            rows = slice(2 * q * DH, (2 * q + 2) * DH)
            lhs = jnp.concatenate([message[where[j], rows, :] for j in range(NT)], axis=1)
            got = dot(lhs, jnp.concatenate([e.astype(BF) for e in weights], axis=0))
            agg[2 * q * DH : (2 * q + 1) * DH, :] = got[:DH, :TILE] * inv[:, :TILE]
            agg[(2 * q + 1) * DH : (2 * q + 2) * DH, :] = got[DH:, TILE:] * inv[:, TILE:]
        merged = agg[...]
        active = (0.5 * merged * (1.0 + lax.erf(merged * math.sqrt(0.5)))).astype(BF).T
        tb = tab[OTYPE + b]
        projected = dot(active, wqo[tb])
        a = jax.nn.sigmoid(jnp.full((1, D), gate[tb], F32))
        for rt in range(2):
            at = slice(rt * HALF, (rt + 1) * HALF)
            own = near0[rt, b].astype(F32)
            send[rt, b] = (a * projected[at] + (1.0 - a) * own).astype(BF)
        return c

    lax.fori_loop(0, NB, attend, 0)
    done = [
        pltpu.make_async_copy(
            send.at[rt, pl.ds(0, NB)], out.at[:, pl.ds(rt * HALF, HALF), :], esem.at[rt]
        )
        for rt in range(2)
    ]
    for c in done:
        c.start()
    for c in done:
        c.wait()


def layer(tiles, types, relation, prior, gate, feats, wq, wk, wv, wo, att, msg):
    smem = pl.BlockSpec(memory_space=pltpu.SMEM)
    hbm = pl.BlockSpec(memory_space=pl.ANY)
    return pl.pallas_call(
        layer_kernel,
        name="layer",
        out_shape=jax.ShapeDtypeStruct((NB, TILE, D), BF),
        in_specs=[smem] * 5 + [hbm] * 7,
        out_specs=hbm,
        scratch_shapes=[
            pltpu.SMEM((TABLE,), jnp.int32),
            *[pltpu.VMEM((2, NB, HALF, D), BF)] * 4,
            pltpu.VMEM((2, 36, HALF, D), BF),
            pltpu.VMEM((2, 36, HALF, D), BF),
            pltpu.VMEM((2, 36, HALF, D), BF),
            pltpu.VMEM((2, 12, HALF, D), BF),
            pltpu.VMEM((3, D, D), BF),
            pltpu.VMEM((3, D, D), BF),
            pltpu.VMEM((3, D, D), BF),
            pltpu.VMEM((NREL, D, DH), BF),
            pltpu.VMEM((NREL, STRIPS, WIN), BF),
            pltpu.VMEM((NREL, STRIPS, WIN), BF),
            pltpu.VMEM((NB, D, TILE), BF),
            pltpu.VMEM((REQ, TILE, D), BF),
            pltpu.VMEM((REQ, D, TILE), BF),
            pltpu.VMEM((HEADS // 2, WIN, WIN), BF),
            pltpu.VMEM((D, TILE), F32),
            pltpu.SemaphoreType.DMA((2,)),
            pltpu.SemaphoreType.DMA((6,)),
            pltpu.SemaphoreType.DMA((2,)),
            pltpu.SemaphoreType.DMA((2, 2, 3)),
            pltpu.SemaphoreType.DMA((2, 2, 3)),
            pltpu.SemaphoreType.DMA((2, 4, 4)),
            pltpu.SemaphoreType.DMA((2, 4, 4)),
        ],
        compiler_params=pltpu.CompilerParams(
            collective_id=0, has_side_effects=True, vmem_limit_bytes=67043328
        ),
    )(tiles, types, relation, prior, gate, feats, wq, wk, wv, wo, att, msg)


def contrast_kernel(
    types, sched, weight, emb, pos, loss, mean, offer, negs, part, lanes, doms, ss, rs, sl, rl, sd, rd
):
    y = lax.axis_index("dom_0")
    core = lax.axis_index("dom_1")
    z = lax.axis_index("narrow_0")
    x = lax.axis_index("narrow_1")
    lane = z * RING + x
    dom = y * 2 + core

    def lane_id(by):
        other = (lane + by) % LANES
        return {"narrow_0": other // RING, "narrow_1": other % RING}

    def dom_id(by):
        other = (dom + by) % 8
        return {"dom_0": other // 2, "dom_1": other % 2}

    barrier = pltpu.get_barrier_semaphore()
    for by in range(1, LANES):
        pl.semaphore_signal(barrier, 1, device_id=lane_id(by), device_id_type=MESH)
    for by in range(1, 8):
        pl.semaphore_signal(barrier, 1, device_id=dom_id(by), device_id_type=MESH)
    pl.semaphore_wait(barrier, LANES - 1 + 7)

    def give(s):
        return pltpu.make_async_remote_copy(
            src_ref=offer.at[s],
            dst_ref=negs.at[s],
            send_sem=ss.at[s],
            recv_sem=rs.at[s],
            device_id=lane_id(s + 1),
            device_id_type=MESH,
        )

    for s in range(STEPS):
        offer[s] = emb[sched[s, lane]]
        give(s).start()
    for s in range(STEPS):
        give(s).wait_recv()

    inv = 1.0 / math.sqrt(D)
    kinds = []
    for s in range(STEPS):
        frm = (lane + LANES - s - 1) % LANES
        kinds.append(types[frm * NB + sched[s, frm]])
    total = jnp.zeros((1, TILE), F32)
    for b in range(NB):
        own = emb[b]
        tb = types[lane * NB + b]
        prod = own.astype(F32) * pos[b].astype(F32)
        fold = prod[:, 0:TILE]
        for c in range(1, D // TILE):
            fold = fold + prod[:, c * TILE : (c + 1) * TILE]
        positive = jnp.sum(fold.T, axis=0, keepdims=True) * inv
        logits = []
        high = positive
        for s in range(STEPS):
            v = dot_t(negs[s], own) * inv
            v = jnp.where(kinds[s] == tb, v, -jnp.inf)
            high = jnp.maximum(high, jnp.max(v, axis=0, keepdims=True))
            logits.append(v)
        den = jnp.exp(positive - high)
        for v in logits:
            den = den + jnp.sum(jnp.exp(v - high), axis=0, keepdims=True)
        row = high + jnp.log(den) - positive
        loss[b : b + 1, :] = row
        total = total + row * weight[tb]
    part[...] = jnp.broadcast_to(total, (8, TILE))

    def lane_copy(by):
        return pltpu.make_async_remote_copy(
            src_ref=part,
            dst_ref=lanes.at[by],
            send_sem=sl.at[by],
            recv_sem=rl.at[by],
            device_id=lane_id(by),
            device_id_type=MESH,
        )

    for by in range(1, LANES):
        lane_copy(by).start()
    lanes[0] = part[...]
    for by in range(1, LANES):
        lane_copy(by).wait_recv()
    for by in range(1, LANES):
        lane_copy(by).wait_send()
    acc = lanes[lane]
    for a in range(1, LANES):
        acc = acc + lanes[(lane - a + LANES) % LANES]
    doms[0] = acc

    def dom_copy(by):
        return pltpu.make_async_remote_copy(
            src_ref=doms.at[0],
            dst_ref=doms.at[by],
            send_sem=sd.at[by],
            recv_sem=rd.at[by],
            device_id=dom_id(by),
            device_id_type=MESH,
        )

    for by in range(1, 8):
        dom_copy(by).start()
    for by in range(1, 8):
        dom_copy(by).wait_recv()
    acc = doms[dom]
    for a in range(1, 8):
        acc = acc + doms[(dom - a + 8) % 8]
    whole = jnp.sum(acc, axis=1, keepdims=True) * (1.0 / (NB * TILE * 128))
    mean[...] = jnp.broadcast_to(whole, (8, TILE))
    for by in range(1, 8):
        dom_copy(by).wait_send()
    for s in range(STEPS):
        give(s).wait_send()


def contrast(types, sched, weight, emb, pos):
    smem = pl.BlockSpec(memory_space=pltpu.SMEM)
    vmem = pl.BlockSpec(memory_space=pltpu.VMEM)
    return pl.pallas_call(
        contrast_kernel,
        name="contrast",
        out_shape=(
            jax.ShapeDtypeStruct((NB, TILE), F32),
            jax.ShapeDtypeStruct((8, TILE), F32),
        ),
        in_specs=[smem, smem, smem, vmem, vmem],
        out_specs=(vmem, vmem),
        scratch_shapes=[
            pltpu.VMEM((STEPS, TILE, D), BF),
            pltpu.VMEM((STEPS, TILE, D), BF),
            pltpu.VMEM((8, TILE), F32),
            pltpu.VMEM((LANES, 8, TILE), F32),
            pltpu.VMEM((8, 8, TILE), F32),
            pltpu.SemaphoreType.DMA((STEPS,)),
            pltpu.SemaphoreType.DMA((STEPS,)),
            pltpu.SemaphoreType.DMA((LANES,)),
            pltpu.SemaphoreType.DMA((LANES,)),
            pltpu.SemaphoreType.DMA((8,)),
            pltpu.SemaphoreType.DMA((8,)),
        ],
        compiler_params=pltpu.CompilerParams(
            collective_id=1, has_side_effects=True, vmem_limit_bytes=60 << 20
        ),
    )(types, sched, weight, emb, pos)


def shards(
    feats,
    node_type,
    tiles,
    relation,
    neg_sched,
    w_query,
    w_key,
    w_value,
    w_out,
    rel_att,
    rel_msg,
    rel_prior,
    skip_gate,
    pos_view,
    type_weight,
):
    blocks = feats.reshape(NB, TILE, D)
    emb = layer(
        tiles.T,
        node_type,
        relation.T,
        rel_prior,
        skip_gate,
        blocks,
        w_query,
        w_key,
        w_value,
        w_out,
        rel_att.reshape(NREL, D, DH),
        rel_msg.reshape(NREL, D, DH),
    )
    loss, mean = contrast(
        node_type, neg_sched.T, type_weight, emb, pos_view.reshape(NB, TILE, D)
    )
    return emb.reshape(NB * TILE, D), loss.reshape(NB * TILE), mean[0, 0]


def solution(mesh):
    finer = Mesh(mesh.devices.reshape(4, 2, 4, 4), DOM_NARROW)
    in_specs = (
        P(DOM_NARROW, None),
        P(DOM),
        P(DOM, None),
        P(DOM_NARROW, None),
        P(DOM, None),
        P(),
        P(),
        P(),
        P(),
        P(),
        P(),
        P(),
        P(),
        P(DOM_NARROW, None),
        P(),
    )
    out_specs = (P(DOM_NARROW, None), P(DOM_NARROW), P())
    return jax.shard_map(
        shards, mesh=finer, in_specs=in_specs, out_specs=out_specs, check_vma=False
    )
```

time: 215 us -> 173 us (0.80)
  Pallas kernels: 206 us -> 168 us
  local copies, waits for them, and re-layouts: 7.96 us -> 3.6 us
    pallas_call x3 -> x1, Pallas kernels: 151 us -> 112 us  [layer(): pl.pallas_call(layer_kernel, name='layer', out_shape=jax.ShapeDtypeStruct...]
    reshape x4 -> x0, local copies, waits for them, and re-layouts: 3.22 us -> none  [the longest x1 1.34 us: shards(): rel_prior.reshape(-1)]
where the time goes in v2:
time: 173 us
  Pallas kernels  168 us (97%)
  local copies, waits for them, and re-layouts  3.6 us (2%)
    pallas_call x1, Pallas kernels, layer(): pl.pallas_call(layer_kernel, name='layer', out_shape=jax.ShapeDtypeStruct...  112 us
    pallas_call x1, Pallas kernels, contrast(): pl.pallas_call(contrast_kernel, name='contrast', out_shape=(jax.ShapeDtyp...  56.4 us

profile of v2, /device:TPU:1, one launch (start us, length us, event | category | flops | bytes accessed | tf_op | source)
XLA Modules:
  0.0 172.6 jit_solution(15199615796046452586)
XLA Ops:
  0.6 112.0 %layer.1.emb = bf16[8,128,768]{2,1,0:T(8,128)(2,1)} custom-call(s32[4,128]{1,0:T(4,128)} %bitcast.17, s32[128]{0:T(128)} %types.3, s32[4,8]{1,0:T(4,128)} %bitcast.18, f32[5,8]{1,0:T(8,128)} %prior.1, f32[3]{0:T(128)} %gate.1, bf16[8,128,768]{2,1,0:T(8,128)(2,1)} %bitcast.11, bf16[3,768,768]{2,1,0:T(8,128)(2,1)} %wq.1, bf16[3,768,768]{2,1,0:T(8,128)(2,1)} %wk.1, ...), custom_call_target="tpu_custom_call" | custom-call | tf_op jit(solution)/shard_map/layer/pallas_call | solution.py:428
  112.6 0.0 copy-start
  112.6 56.4 %contrast.1 = (f32[8,128]{1,0:T(8,128)}, f32[8,128]{1,0:T(8,128)}) custom-call(s32[128]{0:T(128)} %types.3, s32[8,16]{1,0:T(8,128)} %bitcast.15, f32[3]{0:T(128)} %weight.1, bf16[8,128,768]{2,1,0:T(8,128)(2,1)} %layer.1.emb, bf16[8,128,768]{2,1,0:T(8,128)(2,1)} %bitcast.12), custom_call_target="tpu_custom_call" | custom-call | tf_op jit(solution)/shard_map/contrast/pallas_call | solution.py:586
  169.0 1.2 slice.3
  170.2 0.0 copy-done
  170.2 1.1 copy.20
  171.4 1.3 copy.21
Async XLA Ops:
  112.6 57.6 %copy-start = (bf16[8,128,768]{2,1,0:T(8,128)(2,1)S(1)}, bf16[8,128,768]{2,1,0:T(8,128)(2,1)}, u32[]{:S(2)}) copy-start(bf16[8,128,768]{2,1,0:T(8,128)(2,1)} %layer.1.emb) | copy-start | bytes 4718596

commit v3 on v2

--- a/solution.py
+++ b/solution.py
@@ -38,7 +38,10 @@
 ORDER = 232
 STAGE = 264
 OTYPE = 296
-TABLE = 304
+FIRST = 304
+TURN = 312
+BLOCK = 320
+TABLE = 328
 READY = [11, 17, 23, 32]
 STAGE_OF = {(1, 3): 1, (3, 1): 1, (2, 3): 2, (3, 2): 2, (1, 2): 3, (2, 1): 3, (2, 2): 3}
 STRIP_AT = [0, 384, 896]
@@ -81,11 +84,12 @@
 
 
 def layer_kernel(
-    tiles, types, relation, prior, gate, feats, wq, wk, wv, wo, att, msg,
-    out,
+    tiles, types, relation, sched, prior, gate, weight, feats, pos, wq, wk, wv, wo, att, msg,
+    out, loss, mean,
     tab, near0, near1, near2, near3, far, held, send, transit,
     wqo, wks, wvs, raw, att_wide, msg_wide, turned, keyed, message, pairs, agg,
-    lsem, wsem, esem, s1, r1, s2, r2,
+    negs, via, positive, rows_of, subtotal, lanes, doms,
+    lsem, wsem, esem, s1, r1, s2, r2, s3, r3, sl, rl, sd, rd,
 ):
     z = lax.axis_index("narrow_0")
     x = lax.axis_index("narrow_1")
@@ -103,11 +107,22 @@
     ]
     for c in local:
         c.start()
+    dom = lax.axis_index("dom_0") * 2 + lax.axis_index("dom_1")
+
+    def lane_id(by):
+        other = (lane + by) % LANES
+        return {"narrow_0": other // RING, "narrow_1": other % RING}
+
+    def dom_id(by):
+        other = (dom + by) % 8
+        return {"dom_0": other // 2, "dom_1": other % 2}
+
     barrier = pltpu.get_barrier_semaphore()
-    for axis in range(2):
-        for by in (1, 3):
-            pl.semaphore_signal(barrier, 1, device_id=to(axis, by), device_id_type=MESH)
-    pl.semaphore_wait(barrier, 4)
+    for by in range(1, LANES):
+        pl.semaphore_signal(barrier, 1, device_id=lane_id(by), device_id_type=MESH)
+    for by in range(1, 8):
+        pl.semaphore_signal(barrier, 1, device_id=dom_id(by), device_id_type=MESH)
+    pl.semaphore_wait(barrier, LANES - 1 + 7)
     for c in local:
         c.wait()
 
@@ -278,6 +293,20 @@
     lax.fori_loop(0, REQ, invert, 0)
     for b in range(NB):
         tab[OTYPE + b] = types[lane * NB + b]
+        at = jnp.int32(STEPS + b)
+        for n in reversed(range(STEPS)):
+            at = jnp.where(sched[STEPS - 1 - n, lane] == b, n, at)
+        tab[FIRST + b] = at
+    for b in range(NB):
+        ahead = jnp.int32(0)
+        for e in range(NB):
+            ahead = ahead + jnp.where(tab[FIRST + e] < tab[FIRST + b], 1, 0)
+        tab[TURN + b] = ahead
+    for n in range(NB):
+        found = jnp.int32(0)
+        for b in range(NB):
+            found = jnp.where(tab[TURN + b] == n, b, found)
+        tab[BLOCK + n] = found
     pairs[...] = jnp.zeros_like(pairs)
 
     def widen_all(wide):
@@ -297,9 +326,10 @@
 
     load_wq.wait()
 
-    def ask_query(b, c):
+    def ask_query(n, c):
+        b = tab[BLOCK + n]
         rows = jnp.concatenate([near0[0, b], near0[1, b]], axis=0)
-        turned[b] = dot(rows, wqo[tab[OTYPE + b]]).astype(BF).T
+        turned[n] = dot(rows, wqo[tab[OTYPE + b]]).astype(BF).T
         return c
 
     lax.fori_loop(0, NB, ask_query, 0)
@@ -367,16 +397,26 @@
             onward(rt, o).wait_send()
     load_wo.wait()
 
+    load_pos = [
+        pltpu.make_async_copy(
+            pos.at[:, pl.ds(rt * HALF, HALF), :], far.at[rt, pl.ds(0, NB)], lsem.at[rt]
+        )
+        for rt in range(2)
+    ]
+    for c in load_pos:
+        c.start()
+
     left = lax.broadcasted_iota(jnp.int32, (1, WIN), 1) < TILE
     unit = math.log2(math.e) / math.sqrt(DH)
 
-    def attend(b, c):
+    def attend(n, c):
+        b = tab[BLOCK + n]
         where = [tab[PLACE + b * NT + j] for j in range(NT)]
         rel = [tab[RELA + b * NT + j] for j in range(NT)]
         for h in range(HEADS):
             lo = h * DH - PAIR[h // 2]
             pairs[h // 2, lo : lo + DH, h % 2 * TILE : (h % 2 + 1) * TILE] = turned[
-                b, h * DH : (h + 1) * DH, :
+                n, h * DH : (h + 1) * DH, :
             ]
         for q in range(HEADS // 2):
             w = PAIR[q]
@@ -403,34 +443,197 @@
         tb = tab[OTYPE + b]
         projected = dot(active, wqo[tb])
         a = jax.nn.sigmoid(jnp.full((1, D), gate[tb], F32))
+        own = jnp.concatenate([near0[0, b], near0[1, b]], axis=0).astype(F32)
+        emb = (a * projected + (1.0 - a) * own).astype(BF)
+        held[0, n] = emb[:HALF]
+        held[1, n] = emb[HALF:]
+        turned[n] = emb.T
+
+    def relayed(hop):
+        return pltpu.make_async_remote_copy(
+            src_ref=send.at[0, pl.ds(0, 2)] if hop == 0 else via,
+            dst_ref=via if hop == 0 else negs.at[STEPS - 1],
+            send_sem=s3.at[STEPS - 1 + hop],
+            recv_sem=r3.at[STEPS - 1 + hop],
+            device_id=to(1, 3),
+            device_id_type=MESH,
+        )
+
+    def give(n):
+        s = STEPS - 1 - n
+        return pltpu.make_async_remote_copy(
+            src_ref=send.at[0, pl.ds(2 * n, 2)],
+            dst_ref=negs.at[s],
+            send_sem=s3.at[s],
+            recv_sem=r3.at[s],
+            device_id=lane_id(s + 1),
+            device_id_type=MESH,
+        )
+
+    def one_block(n, c):
+        attend(n, c)
+        turn_of = tab[TURN + sched[STEPS - 1 - n, lane]]
+        send[0, 2 * n] = held[0, turn_of]
+        send[0, 2 * n + 1] = held[1, turn_of]
+
+        @pl.when(n == 0)
+        def _():
+            relayed(0).start()
+
+        @pl.when(n > 0)
+        def _():
+            give(n).start()
+
+        @pl.when(n == 4)
+        def _():
+            relayed(0).wait_recv()
+            relayed(1).start()
+
+        return c
+
+    lax.fori_loop(0, NB, one_block, 0)
+
+    for b in range(NB):
         for rt in range(2):
-            at = slice(rt * HALF, (rt + 1) * HALF)
-            own = near0[rt, b].astype(F32)
-            send[rt, b] = (a * projected[at] + (1.0 - a) * own).astype(BF)
-        return c
-
-    lax.fori_loop(0, NB, attend, 0)
+            send[1, 2 * b + rt] = held[rt, tab[TURN + b]]
     done = [
         pltpu.make_async_copy(
-            send.at[rt, pl.ds(0, NB)], out.at[:, pl.ds(rt * HALF, HALF), :], esem.at[rt]
-        )
+            send.at[1, pl.ds(2 * b + rt, 1)],
+            out.at[pl.ds(b, 1), pl.ds(rt * HALF, HALF), :],
+            esem.at[2 * b + rt],
+        )
+        for b in range(NB)
         for rt in range(2)
     ]
     for c in done:
         c.start()
+    for c in load_pos:
+        c.wait()
+
+    scale = 1.0 / math.sqrt(D)
+    for b in range(NB):
+        turn_of = tab[TURN + b]
+        fold = jnp.zeros((TILE, TILE), F32)
+        own = jnp.concatenate([held[0, turn_of], held[1, turn_of]], axis=0).astype(F32)
+        near_by = jnp.concatenate([far[0, b], far[1, b]], axis=0).astype(F32)
+        prod = own * near_by
+        for k in range(D // TILE):
+            fold = fold + prod[:, k * TILE : (k + 1) * TILE]
+        row = jnp.sum(fold.T, axis=0, keepdims=True) * scale
+        positive[b] = jnp.broadcast_to(row, (8, TILE))
+
+    own_type = [tab[OTYPE + tab[BLOCK + n]] for n in range(NB)]
+    base = [
+        jnp.concatenate(
+            [positive[tab[BLOCK + n]][0:1], positive[tab[BLOCK + n + 1]][0:1]],
+            axis=1,
+        )
+        for n in range(0, NB, 2)
+    ]
+
+    def against(s, state):
+        frm = (lane + LANES - s - 1) % LANES
+        kind = types[frm * NB + sched[s, frm]]
+        both = jnp.concatenate([negs[s, 0], negs[s, 1]], axis=0)
+        new = []
+        for m in range(NB // 2):
+            high, den = state[2 * m], state[2 * m + 1]
+            emb = jnp.concatenate([turned[2 * m], turned[2 * m + 1]], axis=1)
+            even = jnp.where(own_type[2 * m] == kind, 0.0, -jnp.inf)
+            odd = jnp.where(own_type[2 * m + 1] == kind, 0.0, -jnp.inf)
+            v = dot(both, emb) * scale + jnp.where(left, even, odd)
+            top = jnp.maximum(high, jnp.max(v, axis=0, keepdims=True))
+            den = den * jnp.exp(high - top) + jnp.sum(jnp.exp(v - top), axis=0, keepdims=True)
+            new += [top, den]
+        return tuple(new)
+
+    state = []
+    for m in range(NB // 2):
+        state += [base[m], jnp.ones((1, WIN), F32)]
+    for s in reversed(range(STEPS - 1)):
+        give(STEPS - 1 - s).wait_recv()
+        state = against(s, state)
+    relayed(1).wait_recv()
+    state = against(STEPS - 1, state)
+
+    total = jnp.zeros((1, TILE), F32)
+    for m in range(NB // 2):
+        row = state[2 * m] + jnp.log(state[2 * m + 1]) - base[m]
+        for i in range(2):
+            n = 2 * m + i
+            one = row[:, i * TILE : (i + 1) * TILE]
+            total = total + one * weight[own_type[n]]
+            rows_of[n] = jnp.broadcast_to(one, (8, TILE))
+    subtotal[...] = jnp.broadcast_to(total, (8, TILE))
+
+    def lane_copy(by):
+        return pltpu.make_async_remote_copy(
+            src_ref=subtotal,
+            dst_ref=lanes.at[by],
+            send_sem=sl.at[by],
+            recv_sem=rl.at[by],
+            device_id=lane_id(by),
+            device_id_type=MESH,
+        )
+
+    for by in range(1, LANES):
+        lane_copy(by).start()
+    for b in range(NB):
+        loss[b : b + 1, :] = rows_of[tab[TURN + b]][0:1]
+    lanes[0] = subtotal[...]
+    for by in range(1, LANES):
+        lane_copy(by).wait_recv()
+    acc = lanes[lane]
+    for k in range(1, LANES):
+        acc = acc + lanes[(lane + LANES - k) % LANES]
+    doms[0] = acc
+
+    def dom_copy(by):
+        return pltpu.make_async_remote_copy(
+            src_ref=doms.at[0],
+            dst_ref=doms.at[by],
+            send_sem=sd.at[by],
+            recv_sem=rd.at[by],
+            device_id=dom_id(by),
+            device_id_type=MESH,
+        )
+
+    for by in range(1, 8):
+        dom_copy(by).start()
     for c in done:
         c.wait()
-
-
-def layer(tiles, types, relation, prior, gate, feats, wq, wk, wv, wo, att, msg):
+    relayed(0).wait_send()
+    relayed(1).wait_send()
+    for n in range(1, STEPS):
+        give(n).wait_send()
+    for by in range(1, LANES):
+        lane_copy(by).wait_send()
+    for by in range(1, 8):
+        dom_copy(by).wait_recv()
+    acc = doms[dom]
+    for k in range(1, 8):
+        acc = acc + doms[(dom + 8 - k) % 8]
+    whole = jnp.sum(acc, axis=1, keepdims=True) * (1.0 / (NB * TILE * 128))
+    mean[...] = jnp.broadcast_to(whole, (8, TILE))
+    for by in range(1, 8):
+        dom_copy(by).wait_send()
+
+
+def layer(*operands):
     smem = pl.BlockSpec(memory_space=pltpu.SMEM)
+    vmem = pl.BlockSpec(memory_space=pltpu.VMEM)
     hbm = pl.BlockSpec(memory_space=pl.ANY)
+    dma = pltpu.SemaphoreType.DMA
     return pl.pallas_call(
         layer_kernel,
         name="layer",
-        out_shape=jax.ShapeDtypeStruct((NB, TILE, D), BF),
-        in_specs=[smem] * 5 + [hbm] * 7,
-        out_specs=hbm,
+        out_shape=(
+            jax.ShapeDtypeStruct((NB, TILE, D), BF),
+            jax.ShapeDtypeStruct((NB, TILE), F32),
+            jax.ShapeDtypeStruct((8, TILE), F32),
+        ),
+        in_specs=[smem] * 7 + [hbm] * 8,
+        out_specs=(hbm, vmem, vmem),
         scratch_shapes=[
             pltpu.SMEM((TABLE,), jnp.int32),
             *[pltpu.VMEM((2, NB, HALF, D), BF)] * 4,
@@ -449,166 +652,31 @@
             pltpu.VMEM((REQ, D, TILE), BF),
             pltpu.VMEM((HEADS // 2, WIN, WIN), BF),
             pltpu.VMEM((D, TILE), F32),
-            pltpu.SemaphoreType.DMA((2,)),
-            pltpu.SemaphoreType.DMA((6,)),
-            pltpu.SemaphoreType.DMA((2,)),
-            pltpu.SemaphoreType.DMA((2, 2, 3)),
-            pltpu.SemaphoreType.DMA((2, 2, 3)),
-            pltpu.SemaphoreType.DMA((2, 4, 4)),
-            pltpu.SemaphoreType.DMA((2, 4, 4)),
+            pltpu.VMEM((STEPS, 2, HALF, D), BF),
+            pltpu.VMEM((2, HALF, D), BF),
+            pltpu.VMEM((NB, 8, TILE), F32),
+            pltpu.VMEM((NB, 8, TILE), F32),
+            pltpu.VMEM((8, TILE), F32),
+            pltpu.VMEM((LANES, 8, TILE), F32),
+            pltpu.VMEM((8, 8, TILE), F32),
+            dma((2,)),
+            dma((6,)),
+            dma((2 * NB,)),
+            dma((2, 2, 3)),
+            dma((2, 2, 3)),
+            dma((2, 4, 4)),
+            dma((2, 4, 4)),
+            dma((STEPS + 1,)),
+            dma((STEPS + 1,)),
+            dma((LANES,)),
+            dma((LANES,)),
+            dma((8,)),
+            dma((8,)),
         ],
         compiler_params=pltpu.CompilerParams(
             collective_id=0, has_side_effects=True, vmem_limit_bytes=67043328
         ),
-    )(tiles, types, relation, prior, gate, feats, wq, wk, wv, wo, att, msg)
-
-
-def contrast_kernel(
-    types, sched, weight, emb, pos, loss, mean, offer, negs, part, lanes, doms, ss, rs, sl, rl, sd, rd
-):
-    y = lax.axis_index("dom_0")
-    core = lax.axis_index("dom_1")
-    z = lax.axis_index("narrow_0")
-    x = lax.axis_index("narrow_1")
-    lane = z * RING + x
-    dom = y * 2 + core
-
-    def lane_id(by):
-        other = (lane + by) % LANES
-        return {"narrow_0": other // RING, "narrow_1": other % RING}
-
-    def dom_id(by):
-        other = (dom + by) % 8
-        return {"dom_0": other // 2, "dom_1": other % 2}
-
-    barrier = pltpu.get_barrier_semaphore()
-    for by in range(1, LANES):
-        pl.semaphore_signal(barrier, 1, device_id=lane_id(by), device_id_type=MESH)
-    for by in range(1, 8):
-        pl.semaphore_signal(barrier, 1, device_id=dom_id(by), device_id_type=MESH)
-    pl.semaphore_wait(barrier, LANES - 1 + 7)
-
-    def give(s):
-        return pltpu.make_async_remote_copy(
-            src_ref=offer.at[s],
-            dst_ref=negs.at[s],
-            send_sem=ss.at[s],
-            recv_sem=rs.at[s],
-            device_id=lane_id(s + 1),
-            device_id_type=MESH,
-        )
-
-    for s in range(STEPS):
-        offer[s] = emb[sched[s, lane]]
-        give(s).start()
-    for s in range(STEPS):
-        give(s).wait_recv()
-
-    inv = 1.0 / math.sqrt(D)
-    kinds = []
-    for s in range(STEPS):
-        frm = (lane + LANES - s - 1) % LANES
-        kinds.append(types[frm * NB + sched[s, frm]])
-    total = jnp.zeros((1, TILE), F32)
-    for b in range(NB):
-        own = emb[b]
-        tb = types[lane * NB + b]
-        prod = own.astype(F32) * pos[b].astype(F32)
-        fold = prod[:, 0:TILE]
-        for c in range(1, D // TILE):
-            fold = fold + prod[:, c * TILE : (c + 1) * TILE]
-        positive = jnp.sum(fold.T, axis=0, keepdims=True) * inv
-        logits = []
-        high = positive
-        for s in range(STEPS):
-            v = dot_t(negs[s], own) * inv
-            v = jnp.where(kinds[s] == tb, v, -jnp.inf)
-            high = jnp.maximum(high, jnp.max(v, axis=0, keepdims=True))
-            logits.append(v)
-        den = jnp.exp(positive - high)
-        for v in logits:
-            den = den + jnp.sum(jnp.exp(v - high), axis=0, keepdims=True)
-        row = high + jnp.log(den) - positive
-        loss[b : b + 1, :] = row
-        total = total + row * weight[tb]
-    part[...] = jnp.broadcast_to(total, (8, TILE))
-
-    def lane_copy(by):
-        return pltpu.make_async_remote_copy(
-            src_ref=part,
-            dst_ref=lanes.at[by],
-            send_sem=sl.at[by],
-            recv_sem=rl.at[by],
-            device_id=lane_id(by),
-            device_id_type=MESH,
-        )
-
-    for by in range(1, LANES):
-        lane_copy(by).start()
-    lanes[0] = part[...]
-    for by in range(1, LANES):
-        lane_copy(by).wait_recv()
-    for by in range(1, LANES):
-        lane_copy(by).wait_send()
-    acc = lanes[lane]
-    for a in range(1, LANES):
-        acc = acc + lanes[(lane - a + LANES) % LANES]
-    doms[0] = acc
-
-    def dom_copy(by):
-        return pltpu.make_async_remote_copy(
-            src_ref=doms.at[0],
-            dst_ref=doms.at[by],
-            send_sem=sd.at[by],
-            recv_sem=rd.at[by],
-            device_id=dom_id(by),
-            device_id_type=MESH,
-        )
-
-    for by in range(1, 8):
-        dom_copy(by).start()
-    for by in range(1, 8):
-        dom_copy(by).wait_recv()
-    acc = doms[dom]
-    for a in range(1, 8):
-        acc = acc + doms[(dom - a + 8) % 8]
-    whole = jnp.sum(acc, axis=1, keepdims=True) * (1.0 / (NB * TILE * 128))
-    mean[...] = jnp.broadcast_to(whole, (8, TILE))
-    for by in range(1, 8):
-        dom_copy(by).wait_send()
-    for s in range(STEPS):
-        give(s).wait_send()
-
-
-def contrast(types, sched, weight, emb, pos):
-    smem = pl.BlockSpec(memory_space=pltpu.SMEM)
-    vmem = pl.BlockSpec(memory_space=pltpu.VMEM)
-    return pl.pallas_call(
-        contrast_kernel,
-        name="contrast",
-        out_shape=(
-            jax.ShapeDtypeStruct((NB, TILE), F32),
-            jax.ShapeDtypeStruct((8, TILE), F32),
-        ),
-        in_specs=[smem, smem, smem, vmem, vmem],
-        out_specs=(vmem, vmem),
-        scratch_shapes=[
-            pltpu.VMEM((STEPS, TILE, D), BF),
-            pltpu.VMEM((STEPS, TILE, D), BF),
-            pltpu.VMEM((8, TILE), F32),
-            pltpu.VMEM((LANES, 8, TILE), F32),
-            pltpu.VMEM((8, 8, TILE), F32),
-            pltpu.SemaphoreType.DMA((STEPS,)),
-            pltpu.SemaphoreType.DMA((STEPS,)),
-            pltpu.SemaphoreType.DMA((LANES,)),
-            pltpu.SemaphoreType.DMA((LANES,)),
-            pltpu.SemaphoreType.DMA((8,)),
-            pltpu.SemaphoreType.DMA((8,)),
-        ],
-        compiler_params=pltpu.CompilerParams(
-            collective_id=1, has_side_effects=True, vmem_limit_bytes=60 << 20
-        ),
-    )(types, sched, weight, emb, pos)
+    )(*operands)
 
 
 def shards(
@@ -629,22 +697,22 @@
     type_weight,
 ):
     blocks = feats.reshape(NB, TILE, D)
-    emb = layer(
+    emb, loss, mean = layer(
         tiles.T,
         node_type,
         relation.T,
+        neg_sched.T,
         rel_prior,
         skip_gate,
+        type_weight,
         blocks,
+        pos_view.reshape(NB, TILE, D),
         w_query,
         w_key,
         w_value,
         w_out,
         rel_att.reshape(NREL, D, DH),
         rel_msg.reshape(NREL, D, DH),
-    )
-    loss, mean = contrast(
-        node_type, neg_sched.T, type_weight, emb, pos_view.reshape(NB, TILE, D)
     )
     return emb.reshape(NB * TILE, D), loss.reshape(NB * TILE), mean[0, 0]
 

time: 173 us -> 152 us (0.88)
  Pallas kernels: 168 us -> 146 us
    pallas_call x2 -> x1, Pallas kernels: 168 us -> 146 us  [layer(): pl.pallas_call(layer_kernel, name='layer', out_shape=(jax.ShapeDtypeStruc...]
    unnamed x4 -> x2, local copies, waits for them, and re-layouts: 2.41 us -> 3.93 us
where the time goes in v3:
time: 152 us
  Pallas kernels  146 us (96%)
  local copies, waits for them, and re-layouts  5.11 us (3%)
    pallas_call x1, Pallas kernels, layer(): pl.pallas_call(layer_kernel, name='layer', out_shape=(jax.ShapeDtypeStruc...  146 us
    unnamed x2, local copies, waits for them, and re-layouts  3.93 us

profile of v3, /device:TPU:1, one launch (start us, length us, event | category | flops | bytes accessed | tf_op | source)
XLA Modules:
  0.0 152.2 jit_solution(7898140897646539220)
XLA Ops:
  0.6 146.4 %layer.1 = (bf16[8,128,768]{2,1,0:T(8,128)(2,1)}, f32[8,128]{1,0:T(8,128)}, f32[8,128]{1,0:T(8,128)}) custom-call(s32[4,128]{1,0:T(4,128)} %bitcast.17, s32[128]{0:T(128)} %types.1, s32[4,8]{1,0:T(4,128)} %bitcast.18, s32[8,16]{1,0:T(8,128)} %bitcast.15, f32[5,8]{1,0:T(8,128)} %prior.1, f32[3]{0:T(128)} %gate.1, f32[3]{0:T(128)} %weight.1, ...), custom_call_target="tpu_custom_call" | custom-call | tf_op jit(solution)/shard_map/layer/pallas_call | solution.py:627
  147.1 1.2 slice.3
  148.2 2.7 %copy.20 = bf16[1024,768]{1,0:T(8,128)(2,1)} copy(bf16[1024,768]{1,0:T(8,128)(2,1)} %bitcast.12) | data formatting | bytes 3145728
  150.9 1.3 copy.21

commit v4 on v3

--- a/solution.py
+++ b/solution.py
@@ -42,8 +42,10 @@
 TURN = 312
 BLOCK = 320
 TABLE = 328
-READY = [11, 17, 23, 32]
-STAGE_OF = {(1, 3): 1, (3, 1): 1, (2, 3): 2, (3, 2): 2, (1, 2): 3, (2, 1): 3, (2, 2): 3}
+READY = [5, 11, 17, 26, 32]
+STAGE_OF = {
+    (1, 3): 1, (3, 1): 1, (2, 3): 2, (3, 2): 2, (1, 2): 3, (2, 1): 3, (2, 2): 3, (1, 1): 4, (3, 3): 4,
+}
 STRIP_AT = [0, 384, 896]
 STRIPS = 1280
 PAIR = [0, 128, 384, 512]
@@ -89,7 +91,7 @@
     tab, near0, near1, near2, near3, far, held, send, transit,
     wqo, wks, wvs, raw, att_wide, msg_wide, turned, keyed, message, pairs, agg,
     negs, via, positive, rows_of, subtotal, lanes, doms,
-    lsem, wsem, esem, s1, r1, s2, r2, s3, r3, sl, rl, sd, rd,
+    lsem, wsem, esem, s1, r1, s2, r2, s3, r3, s4, r4, sl, rl, sd, rd,
 ):
     z = lax.axis_index("narrow_0")
     x = lax.axis_index("narrow_1")
@@ -176,13 +178,14 @@
             device_id_type=MESH,
         )
 
-    def pick(o):
+    def pick(o, last=0):
         for d in (2, 1, 3):
             for rt in range(2):
                 for k in range(CAP):
                     at = (d - 1) * 12 + o * CAP + k
                     send[rt, at] = near[o][rt, tab[SEL + rt * 36 + at]]
-                second(rt, d, o).start()
+                if d != last:
+                    second(rt, d, o).start()
 
     def take(d, o):
         at = (d - 1) * 12 + o * CAP
@@ -264,17 +267,17 @@
         tab[STYPE + p] = types[t]
         tab[RELA + p] = relation[p % NT, p // NT]
         tab[STAGE + p] = stage
-        for v in range(3):
+        for v in range(4):
             c[LANES + v] = c[LANES + v] + jnp.where(stage <= v, 1, 0)
         return tuple(c)
 
-    counts = lax.fori_loop(0, REQ, mine, (jnp.int32(0),) * (LANES + 3))[LANES:]
+    counts = lax.fori_loop(0, REQ, mine, (jnp.int32(0),) * (LANES + 4))[LANES:]
 
     def turn(p, c):
         c = list(c)
         stage = tab[STAGE + p]
         place = jnp.int32(0)
-        for v in range(4):
+        for v in range(5):
             hit = stage == v
             place = jnp.where(hit, c[v], place)
             c[v] = jnp.where(hit, c[v] + 1, c[v])
@@ -342,8 +345,8 @@
     for rt in range(2):
         for way in range(2):
             first(rt, way, 1).wait_recv()
-    pick(1)
-    pick(3)
+    pick(1, last=1)
+    pick(3, last=3)
     for rt in range(2):
         for way in range(2):
             forward(rt, way).wait_recv()
@@ -368,14 +371,18 @@
         message[n] = spread(value, msg_wide.at[r]).astype(BF).T
         return c
 
-    for d, o in ((3, 0), (1, 0), (2, 0), (3, 1)):
-        take(d, o)
+    take(3, 0)
+    take(1, 0)
+    take(2, 0)
     relay(3)
-    take(3, 3)
+    lax.fori_loop(0, READY[0], transform, 0)
     relay(1)
-    take(1, 1)
-    lax.fori_loop(0, READY[0], transform, 0)
+    for rt in range(2):
+        second(rt, 1, 1).start()
     relay(2)
+    for rt in range(2):
+        second(rt, 3, 3).start()
+    take(3, 1)
     take(1, 3)
     lax.fori_loop(READY[0], READY[1], transform, 0)
     take(3, 2)
@@ -385,6 +392,9 @@
     take(2, 1)
     take(2, 2)
     lax.fori_loop(READY[2], READY[3], transform, 0)
+    take(1, 1)
+    take(3, 3)
+    lax.fori_loop(READY[3], READY[4], transform, 0)
 
     for rt in range(2):
         for way in range(2):
@@ -449,16 +459,6 @@
         held[1, n] = emb[HALF:]
         turned[n] = emb.T
 
-    def relayed(hop):
-        return pltpu.make_async_remote_copy(
-            src_ref=send.at[0, pl.ds(0, 2)] if hop == 0 else via,
-            dst_ref=via if hop == 0 else negs.at[STEPS - 1],
-            send_sem=s3.at[STEPS - 1 + hop],
-            recv_sem=r3.at[STEPS - 1 + hop],
-            device_id=to(1, 3),
-            device_id_type=MESH,
-        )
-
     def give(n):
         s = STEPS - 1 - n
         return pltpu.make_async_remote_copy(
@@ -470,6 +470,26 @@
             device_id_type=MESH,
         )
 
+    def to_via(n):
+        return pltpu.make_async_remote_copy(
+            src_ref=send.at[0, pl.ds(2 * n, 2)],
+            dst_ref=via.at[n],
+            send_sem=s3.at[STEPS - 1 - n],
+            recv_sem=r4.at[n],
+            device_id={"narrow_0": (z + 3) % RING, "narrow_1": (x + RING - n) % RING},
+            device_id_type=MESH,
+        )
+
+    def from_via(n):
+        return pltpu.make_async_remote_copy(
+            src_ref=via.at[n],
+            dst_ref=negs.at[STEPS - 1 - n],
+            send_sem=s4.at[n],
+            recv_sem=r3.at[STEPS - 1 - n],
+            device_id=to(1, 3),
+            device_id_type=MESH,
+        )
+
     def one_block(n, c):
         attend(n, c)
         turn_of = tab[TURN + sched[STEPS - 1 - n, lane]]
@@ -478,16 +498,29 @@
 
         @pl.when(n == 0)
         def _():
-            relayed(0).start()
-
-        @pl.when(n > 0)
+            to_via(0).start()
+
+        @pl.when(jnp.logical_and(n == 1, x > 0))
+        def _():
+            to_via(1).start()
+
+        @pl.when(jnp.logical_and(n == 1, x == 0))
+        def _():
+            give(1).start()
+
+        @pl.when(n > 1)
         def _():
             give(n).start()
 
-        @pl.when(n == 4)
+        @pl.when(n == 3)
         def _():
-            relayed(0).wait_recv()
-            relayed(1).start()
+            to_via(0).wait_recv()
+            from_via(0).start()
+
+        @pl.when(jnp.logical_and(n == 5, x < RING - 1))
+        def _():
+            to_via(1).wait_recv()
+            from_via(1).start()
 
         return c
 
@@ -550,11 +583,9 @@
     state = []
     for m in range(NB // 2):
         state += [base[m], jnp.ones((1, WIN), F32)]
-    for s in reversed(range(STEPS - 1)):
+    for s in (5, 4, 7, 3, 6, 2, 1, 0):
         give(STEPS - 1 - s).wait_recv()
         state = against(s, state)
-    relayed(1).wait_recv()
-    state = against(STEPS - 1, state)
 
     total = jnp.zeros((1, TILE), F32)
     for m in range(NB // 2):
@@ -602,10 +633,14 @@
         dom_copy(by).start()
     for c in done:
         c.wait()
-    relayed(0).wait_send()
-    relayed(1).wait_send()
-    for n in range(1, STEPS):
+    for n in range(STEPS):
         give(n).wait_send()
+    from_via(0).wait_send()
+
+    @pl.when(x < RING - 1)
+    def _():
+        from_via(1).wait_send()
+
     for by in range(1, LANES):
         lane_copy(by).wait_send()
     for by in range(1, 8):
@@ -653,7 +688,7 @@
             pltpu.VMEM((HEADS // 2, WIN, WIN), BF),
             pltpu.VMEM((D, TILE), F32),
             pltpu.VMEM((STEPS, 2, HALF, D), BF),
-            pltpu.VMEM((2, HALF, D), BF),
+            pltpu.VMEM((2, 2, HALF, D), BF),
             pltpu.VMEM((NB, 8, TILE), F32),
             pltpu.VMEM((NB, 8, TILE), F32),
             pltpu.VMEM((8, TILE), F32),
@@ -666,8 +701,10 @@
             dma((2, 2, 3)),
             dma((2, 4, 4)),
             dma((2, 4, 4)),
-            dma((STEPS + 1,)),
-            dma((STEPS + 1,)),
+            dma((STEPS,)),
+            dma((STEPS,)),
+            dma((2,)),
+            dma((2,)),
             dma((LANES,)),
             dma((LANES,)),
             dma((8,)),
@@ -677,6 +714,45 @@
             collective_id=0, has_side_effects=True, vmem_limit_bytes=67043328
         ),
     )(*operands)
+
+
+def finish_kernel(emb, loss, mean, emb_out, loss_out, mean_out, buf, came, went):
+    def come(i):
+        return pltpu.make_async_copy(emb.at[i], buf.at[i], came.at[i])
+
+    def go(i):
+        return pltpu.make_async_copy(buf.at[i], emb_out.at[i], went.at[i])
+
+    for i in range(NB):
+        come(i).start()
+    loss_out[...] = loss[...]
+    mean_out[...] = mean[0:1, 0:1]
+    for i in range(NB):
+        come(i).wait()
+        go(i).start()
+    for i in range(NB):
+        go(i).wait()
+
+
+def finish(emb, loss, mean):
+    vmem = pl.BlockSpec(memory_space=pltpu.VMEM)
+    hbm = pl.BlockSpec(memory_space=pl.ANY)
+    return pl.pallas_call(
+        finish_kernel,
+        name="finish",
+        out_shape=(
+            jax.ShapeDtypeStruct((NB, TILE, D), BF),
+            jax.ShapeDtypeStruct((NB, TILE), F32),
+            jax.ShapeDtypeStruct((1, 1), F32),
+        ),
+        in_specs=[hbm, vmem, vmem],
+        out_specs=(hbm, vmem, vmem),
+        scratch_shapes=[
+            pltpu.VMEM((NB, TILE, D), BF),
+            pltpu.SemaphoreType.DMA((NB,)),
+            pltpu.SemaphoreType.DMA((NB,)),
+        ],
+    )(emb, loss, mean)
 
 
 def shards(
@@ -714,6 +790,7 @@
         rel_att.reshape(NREL, D, DH),
         rel_msg.reshape(NREL, D, DH),
     )
+    emb, loss, mean = finish(emb, loss, mean)
     return emb.reshape(NB * TILE, D), loss.reshape(NB * TILE), mean[0, 0]
 
 

time: 152 us -> 146 us (0.961)
  local copies, waits for them, and re-layouts: 5.11 us -> 0 us
    pallas_call x1, Pallas kernels: 146 us -> 141 us  [layer(): pl.pallas_call(layer_kernel, name='layer', out_shape=(jax.ShapeDtypeStruc...]
    unnamed x2 -> x0, local copies, waits for them, and re-layouts: 3.93 us -> none
    pallas_call x0 -> x1, Pallas kernels: none -> 3.57 us  [finish(): pl.pallas_call(finish_kernel, name='finish', out_shape=(jax.ShapeDtypeStr...]
where the time goes in v4:
time: 146 us
  Pallas kernels  145 us (99%)
    pallas_call x1, Pallas kernels, layer(): pl.pallas_call(layer_kernel, name='layer', out_shape=(jax.ShapeDtypeStruc...  141 us
    pallas_call x1, Pallas kernels, finish(): pl.pallas_call(finish_kernel, name='finish', out_shape=(jax.ShapeDtypeStr...  3.57 us

profile of v4, /device:TPU:1, one launch (start us, length us, event | category | flops | bytes accessed | tf_op | source)
XLA Modules:
  0.0 145.6 jit_solution(15558224205706801692)
XLA Ops:
  0.6 141.3 %layer.1 = (bf16[8,128,768]{2,1,0:T(8,128)(2,1)}, f32[8,128]{1,0:T(8,128)}, f32[8,128]{1,0:T(8,128)}) custom-call(s32[4,128]{1,0:T(4,128)} %bitcast.15, s32[128]{0:T(128)} %types.1, s32[4,8]{1,0:T(4,128)} %bitcast.16, s32[8,16]{1,0:T(8,128)} %bitcast.14, f32[5,8]{1,0:T(8,128)} %prior.1, f32[3]{0:T(128)} %gate.1, f32[3]{0:T(128)} %weight.1, ...), custom_call_target="tpu_custom_call" | custom-call | tf_op jit(solution)/shard_map/layer/pallas_call | solution.py:662
  141.9 3.6 %finish.1 = (bf16[8,128,768]{2,1,0:T(8,128)(2,1)}, f32[8,128]{1,0:T(8,128)}, f32[1,1]{1,0:T(1,128)}) custom-call(bf16[8,128,768]{2,1,0:T(8,128)(2,1)} %get-tuple-element.9.emb, f32[8,128]{1,0:T(8,128)} %get-tuple-element.10.loss, f32[8,128]{1,0:T(8,128)} %get-tuple-element.11.mean), custom_call_target="tpu_custom_call" | custom-call | tf_op jit(solution)/shard_map/finish/pallas_call | solution.py:740

commit v5 on v4

--- a/solution.py
+++ b/solution.py
@@ -41,8 +41,10 @@
 FIRST = 304
 TURN = 312
 BLOCK = 320
-TABLE = 328
-READY = [5, 11, 17, 26, 32]
+OFFER = 328
+TABLE = 336
+SENT = (4, 8, 5, 7, 6, 3, 2, 1)
+READY = [4, 10, 16, 26, 32]
 STAGE_OF = {
     (1, 3): 1, (3, 1): 1, (2, 3): 2, (3, 2): 2, (1, 2): 3, (2, 1): 3, (2, 2): 3, (1, 1): 4, (3, 3): 4,
 }
@@ -298,7 +300,7 @@
         tab[OTYPE + b] = types[lane * NB + b]
         at = jnp.int32(STEPS + b)
         for n in reversed(range(STEPS)):
-            at = jnp.where(sched[STEPS - 1 - n, lane] == b, n, at)
+            at = jnp.where(sched[SENT[n] - 1, lane] == b, n, at)
         tab[FIRST + b] = at
     for b in range(NB):
         ahead = jnp.int32(0)
@@ -310,6 +312,7 @@
         for b in range(NB):
             found = jnp.where(tab[TURN + b] == n, b, found)
         tab[BLOCK + n] = found
+        tab[OFFER + n] = tab[TURN + sched[SENT[n] - 1, lane]]
     pairs[...] = jnp.zeros_like(pairs)
 
     def widen_all(wide):
@@ -371,11 +374,18 @@
         message[n] = spread(value, msg_wide.at[r]).astype(BF).T
         return c
 
+    def transform_all(start, stop):
+        def two(i, c):
+            transform(2 * i, c)
+            return transform(2 * i + 1, c)
+
+        lax.fori_loop(start // 2, stop // 2, two, 0)
+
     take(3, 0)
     take(1, 0)
     take(2, 0)
     relay(3)
-    lax.fori_loop(0, READY[0], transform, 0)
+    transform_all(0, READY[0])
     relay(1)
     for rt in range(2):
         second(rt, 1, 1).start()
@@ -384,17 +394,17 @@
         second(rt, 3, 3).start()
     take(3, 1)
     take(1, 3)
-    lax.fori_loop(READY[0], READY[1], transform, 0)
+    transform_all(READY[0], READY[1])
     take(3, 2)
     take(2, 3)
-    lax.fori_loop(READY[1], READY[2], transform, 0)
+    transform_all(READY[1], READY[2])
     take(1, 2)
     take(2, 1)
     take(2, 2)
-    lax.fori_loop(READY[2], READY[3], transform, 0)
+    transform_all(READY[2], READY[3])
     take(1, 1)
     take(3, 3)
-    lax.fori_loop(READY[3], READY[4], transform, 0)
+    transform_all(READY[3], READY[4])
 
     for rt in range(2):
         for way in range(2):
@@ -459,68 +469,73 @@
         held[1, n] = emb[HALF:]
         turned[n] = emb.T
 
-    def give(n):
-        s = STEPS - 1 - n
+    def give(step):
         return pltpu.make_async_remote_copy(
-            src_ref=send.at[0, pl.ds(2 * n, 2)],
-            dst_ref=negs.at[s],
-            send_sem=s3.at[s],
-            recv_sem=r3.at[s],
-            device_id=lane_id(s + 1),
+            src_ref=send.at[0, pl.ds(2 * SENT.index(step), 2)],
+            dst_ref=negs.at[step - 1],
+            send_sem=s3.at[step - 1],
+            recv_sem=r3.at[step - 1],
+            device_id=lane_id(step),
             device_id_type=MESH,
         )
 
-    def to_via(n):
+    def to_via(step):
         return pltpu.make_async_remote_copy(
-            src_ref=send.at[0, pl.ds(2 * n, 2)],
-            dst_ref=via.at[n],
-            send_sem=s3.at[STEPS - 1 - n],
-            recv_sem=r4.at[n],
-            device_id={"narrow_0": (z + 3) % RING, "narrow_1": (x + RING - n) % RING},
+            src_ref=send.at[0, pl.ds(2 * SENT.index(step), 2)],
+            dst_ref=via.at[8 - step],
+            send_sem=s3.at[step - 1],
+            recv_sem=r4.at[8 - step],
+            device_id={"narrow_0": (z + 3) % RING, "narrow_1": (x + step) % RING},
             device_id_type=MESH,
         )
 
-    def from_via(n):
+    def from_via(step):
         return pltpu.make_async_remote_copy(
-            src_ref=via.at[n],
-            dst_ref=negs.at[STEPS - 1 - n],
-            send_sem=s4.at[n],
-            recv_sem=r3.at[STEPS - 1 - n],
+            src_ref=via.at[8 - step],
+            dst_ref=negs.at[step - 1],
+            send_sem=s4.at[8 - step],
+            recv_sem=r3.at[step - 1],
             device_id=to(1, 3),
             device_id_type=MESH,
         )
 
     def one_block(n, c):
         attend(n, c)
-        turn_of = tab[TURN + sched[STEPS - 1 - n, lane]]
+        turn_of = tab[OFFER + n]
         send[0, 2 * n] = held[0, turn_of]
         send[0, 2 * n + 1] = held[1, turn_of]
-
-        @pl.when(n == 0)
-        def _():
-            to_via(0).start()
-
-        @pl.when(jnp.logical_and(n == 1, x > 0))
-        def _():
-            to_via(1).start()
-
-        @pl.when(jnp.logical_and(n == 1, x == 0))
-        def _():
-            give(1).start()
-
-        @pl.when(n > 1)
-        def _():
-            give(n).start()
-
-        @pl.when(n == 3)
-        def _():
-            to_via(0).wait_recv()
-            from_via(0).start()
-
-        @pl.when(jnp.logical_and(n == 5, x < RING - 1))
-        def _():
-            to_via(1).wait_recv()
-            from_via(1).start()
+        for i, step in enumerate(SENT):
+            if step == 8:
+
+                @pl.when(n == i)
+                def _():
+                    to_via(8).start()
+
+                @pl.when(n == i + 3)
+                def _():
+                    to_via(8).wait_recv()
+                    from_via(8).start()
+
+            elif step == 7:
+
+                @pl.when(jnp.logical_and(n == i, x > 0))
+                def _():
+                    to_via(7).start()
+
+                @pl.when(jnp.logical_and(n == i, x == 0))
+                def _():
+                    give(7).start()
+
+                @pl.when(jnp.logical_and(n == i + 3, x < RING - 1))
+                def _():
+                    to_via(7).wait_recv()
+                    from_via(7).start()
+
+            else:
+
+                @pl.when(n == i)
+                def _(step=step):
+                    give(step).start()
 
         return c
 
@@ -583,9 +598,9 @@
     state = []
     for m in range(NB // 2):
         state += [base[m], jnp.ones((1, WIN), F32)]
-    for s in (5, 4, 7, 3, 6, 2, 1, 0):
-        give(STEPS - 1 - s).wait_recv()
-        state = against(s, state)
+    for step in (4, 5, 8, 6, 3, 7, 2, 1):
+        give(step).wait_recv()
+        state = against(step - 1, state)
 
     total = jnp.zeros((1, TILE), F32)
     for m in range(NB // 2):
@@ -633,13 +648,13 @@
         dom_copy(by).start()
     for c in done:
         c.wait()
-    for n in range(STEPS):
-        give(n).wait_send()
-    from_via(0).wait_send()
+    for step in SENT:
+        give(step).wait_send()
+    from_via(8).wait_send()
 
     @pl.when(x < RING - 1)
     def _():
-        from_via(1).wait_send()
+        from_via(7).wait_send()
 
     for by in range(1, LANES):
         lane_copy(by).wait_send()

time: 146 us -> 145 us (level)
  no operation moved by 1% of the time
where the time goes in v5:
time: 145 us
  Pallas kernels  144 us (99%)
    pallas_call x1, Pallas kernels, layer(): pl.pallas_call(layer_kernel, name='layer', out_shape=(jax.ShapeDtypeStruc...  140 us
    pallas_call x1, Pallas kernels, finish(): pl.pallas_call(finish_kernel, name='finish', out_shape=(jax.ShapeDtypeStr...  3.57 us

profile of v5, /device:TPU:1, one launch (start us, length us, event | category | flops | bytes accessed | tf_op | source)
XLA Modules:
  0.0 144.7 jit_solution(1962376647369346630)
XLA Ops:
  0.6 140.3 %layer.1 = (bf16[8,128,768]{2,1,0:T(8,128)(2,1)}, f32[8,128]{1,0:T(8,128)}, f32[8,128]{1,0:T(8,128)}) custom-call(s32[4,128]{1,0:T(4,128)} %bitcast.15, s32[128]{0:T(128)} %types.1, s32[4,8]{1,0:T(4,128)} %bitcast.16, s32[8,16]{1,0:T(8,128)} %bitcast.14, f32[5,8]{1,0:T(8,128)} %prior.1, f32[3]{0:T(128)} %gate.1, f32[3]{0:T(128)} %weight.1, ...), custom_call_target="tpu_custom_call" | custom-call | tf_op jit(solution)/shard_map/layer/pallas_call | solution.py:677
  141.0 3.6 %finish.1 = (bf16[8,128,768]{2,1,0:T(8,128)(2,1)}, f32[8,128]{1,0:T(8,128)}, f32[1,1]{1,0:T(1,128)}) custom-call(bf16[8,128,768]{2,1,0:T(8,128)(2,1)} %get-tuple-element.9.emb, f32[8,128]{1,0:T(8,128)} %get-tuple-element.10.loss, f32[8,128]{1,0:T(8,128)} %get-tuple-element.11.mean), custom_call_target="tpu_custom_call" | custom-call | tf_op jit(solution)/shard_map/finish/pallas_call | solution.py:755

commit v6 on v5

--- a/solution.py
+++ b/solution.py
@@ -127,14 +127,12 @@
     for by in range(1, 8):
         pl.semaphore_signal(barrier, 1, device_id=dom_id(by), device_id_type=MESH)
     pl.semaphore_wait(barrier, LANES - 1 + 7)
-    for c in local:
-        c.wait()
 
     def first(rt, way, part):
         by = slot = (1, 3)[way]
         half = part if way == 0 else 1 - part
         return pltpu.make_async_remote_copy(
-            src_ref=near0.at[rt, pl.ds(half * 4, 4)],
+            src_ref=feats.at[pl.ds(half * 4, 4), pl.ds(rt * HALF, HALF), :],
             dst_ref=near[slot].at[rt, pl.ds(half * 4, 4)],
             send_sem=s1.at[rt, way, part],
             recv_sem=r1.at[rt, way, part],
@@ -243,6 +241,8 @@
                     tab[SEL + rt * 36 + (d - 1) * 12 + o * CAP + k] = (
                         got[o] // NB**k
                     ) % NB
+    for c in local:
+        c.wait()
     pick(0)
 
     def mine(p, c):

time: 145 us -> 145 us (level)
  no operation moved by 1% of the time
where the time goes in v6:
time: 145 us
  Pallas kernels  144 us (99%)
    pallas_call x1, Pallas kernels, layer(): pl.pallas_call(layer_kernel, name='layer', out_shape=(jax.ShapeDtypeStruc...  141 us
    pallas_call x1, Pallas kernels, finish(): pl.pallas_call(finish_kernel, name='finish', out_shape=(jax.ShapeDtypeStr...  3.57 us

profile of v6, /device:TPU:1, one launch (start us, length us, event | category | flops | bytes accessed | tf_op | source)
XLA Modules:
  0.0 144.9 jit_solution(14849363005092908684)
XLA Ops:
  0.6 140.5 %layer.1 = (bf16[8,128,768]{2,1,0:T(8,128)(2,1)}, f32[8,128]{1,0:T(8,128)}, f32[8,128]{1,0:T(8,128)}) custom-call(s32[4,128]{1,0:T(4,128)} %bitcast.15, s32[128]{0:T(128)} %types.1, s32[4,8]{1,0:T(4,128)} %bitcast.16, s32[8,16]{1,0:T(8,128)} %bitcast.14, f32[5,8]{1,0:T(8,128)} %prior.1, f32[3]{0:T(128)} %gate.1, f32[3]{0:T(128)} %weight.1, ...), custom_call_target="tpu_custom_call" | custom-call | tf_op jit(solution)/shard_map/layer/pallas_call | solution.py:677
  141.2 3.6 %finish.1 = (bf16[8,128,768]{2,1,0:T(8,128)(2,1)}, f32[8,128]{1,0:T(8,128)}, f32[1,1]{1,0:T(1,128)}) custom-call(bf16[8,128,768]{2,1,0:T(8,128)(2,1)} %get-tuple-element.9.emb, f32[8,128]{1,0:T(8,128)} %get-tuple-element.10.loss, f32[8,128]{1,0:T(8,128)} %get-tuple-element.11.mean), custom_call_target="tpu_custom_call" | custom-call | tf_op jit(solution)/shard_map/finish/pallas_call | solution.py:755
